TPU v7x, 512 devices: a whole 4x4x16 slice. The times are simulated.
512 devices in a mesh: ctx: 32 (over y_lo, z), fsdp: 16 (over x, y_hi, core).
Axes of the slice: x: 4, y: 4 (y_hi: 2, y_lo: 2; y = y_hi * 2 + y_lo), z: 16, core: 2. Of those that a mesh axis runs over, the one named last changes fastest.
Arguments:
- hidden_in: bfloat16 [16, 8192, 4096], P('fsdp', 'ctx'), may hold values from -40 to 40
- page_tokens: int32 [16, 16], P('fsdp'), may hold values from 1 to 1280, 8192 in all within a row
- grad_attn: bfloat16 [16, 8192, 128], P('fsdp', 'ctx'), may hold values from -6 to 6
- w_qkv: bfloat16 [4096, 384], P('fsdp'), may hold values from -1 to 1
Outputs:
- grad_hidden: bfloat16 [16, 8192, 4096], P('fsdp', 'ctx')
- grad_w_qkv: float32 [4096, 384], P('fsdp')
Inputs may be any that keep to these rules, and one draw needn't show every extreme that they name: `page_tokens`: each document's page lengths sum to 8192.
All inputs are finite; a program needn't handle non-finite values.
Results may differ from a plain program's by a relative error of at most 0.039.
Values may be sent and summed in bfloat16 or wider, within the bound.
A program may use at most 128 MiB of HBM per device.

v0:
```python
import jax
import jax.numpy as jnp
from jax import lax
from jax.sharding import PartitionSpec as P


def page_limits(page_row, positions, total_len):
    page_ends = jnp.cumsum(page_row)
    return jnp.min(
        jnp.where(page_ends[None, :] > positions[:, None], page_ends[None, :], total_len), axis=1
    )


def dot_rows(left, right):
    return lax.dot_general(
        left, right, (((1,), (1,)), ((), ())), preferred_element_type=jnp.float32
    )


def dot_cols(left, right):
    return lax.dot_general(
        left, right, (((0,), (0,)), ((), ())), preferred_element_type=jnp.float32
    )


def local(hidden_in, page_tokens, grad_attn, w_qkv):
    inputs_dev = hidden_in[0]
    grad_out = grad_attn[0]
    page_row = page_tokens[0]
    tok_rows = inputs_dev.shape[0]
    head_width = grad_out.shape[1]
    seq_len = tok_rows * lax.axis_size("ctx")
    score_scale = head_width ** (-0.5)
    weights_all = lax.all_gather(w_qkv, "fsdp", axis=0, tiled=True)
    projected = jnp.dot(inputs_dev, weights_all, preferred_element_type=jnp.float32)
    projected = projected.astype(jnp.bfloat16)
    queries = projected[:, :head_width]
    keys_own = projected[:, head_width : 2 * head_width]
    values_own = projected[:, 2 * head_width :]
    keys_all, values_all = (
        lax.all_gather(keys_own, "ctx", axis=0, tiled=True),
        lax.all_gather(values_own, "ctx", axis=0, tiled=True),
    )
    first_pos = lax.axis_index("ctx") * tok_rows
    positions = first_pos + jnp.arange(tok_rows, dtype=jnp.int32)
    limits = page_limits(page_row, positions, seq_len)
    key_pos = jnp.arange(seq_len, dtype=jnp.int32)
    visible = key_pos[None, :] < limits[:, None]
    scores = jnp.where(visible, dot_rows(queries, keys_all) * score_scale, -1e30)
    row_max = jnp.max(scores, axis=1, keepdims=True)
    log_total = row_max[:, 0] + jnp.log(jnp.sum(jnp.exp(scores - row_max), axis=1))
    probs_full = jnp.exp(scores - log_total[:, None])
    probs_half = probs_full.astype(jnp.bfloat16)
    attended = jnp.dot(probs_half, values_all, preferred_element_type=jnp.float32)
    out_dot = jnp.sum(grad_out.astype(jnp.float32) * attended, axis=1)
    dprob = dot_rows(grad_out, values_all)
    dscore = (probs_full * (dprob - out_dot[:, None]) * score_scale).astype(jnp.bfloat16)
    query_grad = jnp.dot(dscore, keys_all, preferred_element_type=jnp.float32)
    q_piece = lax.all_gather(queries.astype(jnp.float32), "ctx", axis=0, tiled=True).astype(
        jnp.bfloat16
    )
    grad_piece = lax.all_gather(grad_out.astype(jnp.float32), "ctx", axis=0, tiled=True).astype(
        jnp.bfloat16
    )
    total_piece = lax.all_gather(log_total, "ctx", axis=0, tiled=True)
    dot_piece = lax.all_gather(out_dot, "ctx", axis=0, tiled=True)
    piece_rows = q_piece.shape[0]
    piece_limits = page_limits(page_row, jnp.arange(piece_rows, dtype=jnp.int32), seq_len)
    seen = positions[None, :] < piece_limits[:, None]
    piece_scores = jnp.where(seen, dot_rows(q_piece, keys_own) * score_scale, -1e30)
    piece_probs = jnp.exp(piece_scores - total_piece[:, None])
    piece_half = piece_probs.astype(jnp.bfloat16)
    piece_dprob = dot_rows(grad_piece, values_own)
    piece_dscore = (piece_probs * (piece_dprob - dot_piece[:, None]) * score_scale).astype(
        jnp.bfloat16
    )
    key_grad = dot_cols(piece_dscore, q_piece)
    value_grad = dot_cols(piece_half, grad_piece)
    grad_qkv = jnp.concatenate([query_grad, key_grad, value_grad], axis=1).astype(jnp.bfloat16)
    grad_inputs = dot_rows(grad_qkv, weights_all)
    grad_inputs = grad_inputs.astype(jnp.bfloat16)[None]
    block_term = dot_cols(inputs_dev, grad_qkv).astype(jnp.bfloat16)
    block_sum = lax.psum_scatter(
        lax.optimization_barrier(block_term).astype(jnp.float32).astype(jnp.bfloat16),
        "fsdp",
        scatter_dimension=0,
        tiled=True,
    ).astype(jnp.float32)
    grad_weights = lax.psum(block_sum, "ctx")
    return (grad_inputs, grad_weights)


def solution(mesh):
    in_specs = (P("fsdp", "ctx", None), P("fsdp", None), P("fsdp", "ctx", None), P("fsdp", None))
    out_specs = (P("fsdp", "ctx", None), P("fsdp", None))
    return jax.shard_map(local, mesh=mesh, in_specs=in_specs, out_specs=out_specs, check_vma=False)
```

profile of v0, /device:TPU:6, one launch (start us, length us, event | category | flops | bytes accessed | tf_op | source)
XLA Modules:
  0.0 845.0 jit_solution(10110642753795459561)
XLA Ops:
  7.2 0.7 all-gather.8.cloned.1.call-update
  8.0 75.1 %all-gather.8.cloned.1.call-done = bf16[4096,384]{1,0:T(8,128)(2,1)} async-done(((bf16[256,384]{1,0:T(8,128)(2,1)}), bf16[4096,384]{1,0:T(8,128)(2,1)}) %all-gather.8.cloned.1.call-update) | async-done | bytes 3145744 | tf_op jit(solution)/shard_map/all_gather | solution.py:34
  83.1 3.1 fusion.25
  87.0 0.7 all-gather.12.cloned.1.call-update
  88.3 0.7 copy.18
  89.7 130.2 %all-gather.10.cloned.1.call-done = bf16[8192,128]{1,0:T(8,128)(2,1)} async-done(((bf16[256,128]{1,0:T(8,128)(2,1)}), bf16[8192,128]{1,0:T(8,128)(2,1)}) %all-gather.10.cloned.1.call-update) | async-done | bytes 2097168 | tf_op jit(solution)/shard_map/all_gather | solution.py:41
  219.9 3.3 fusion.55
  223.2 1.3 exponential_reduce_fusion
  224.6 1.8 copy-done.1
  226.4 123.1 %all-gather.12.cloned.1.call-done = bf16[8192,128]{1,0:T(8,128)(2,1)} async-done(((bf16[256,128]{1,0:T(8,128)(2,1)}), bf16[8192,128]{1,0:T(8,128)(2,1)}) %all-gather.12.cloned.1.call-update) | async-done | bytes 2097168 | tf_op jit(solution)/shard_map/all_gather | solution.py:42
  349.6 5.7 fusion.36
  355.3 61.5 %all-gather.1 = f32[32,1,256]{2,1,0:T(1,128)S(1)} all-gather(f32[1,1,256]{2,1,0:T(1,128)S(1)} %bitcast.63), channel_id=1, replica_groups=mesh['ctx'=32,'fsdp'=16] {'ctx'}, dimensions={0}, use_global_device_ids=true | all-gather | bytes 33792 | tf_op jit(solution)/shard_map/all_gather | solution.py:66
  416.8 58.6 %all-gather = f32[32,1,256]{2,1,0:T(1,128)S(1)} all-gather(f32[1,1,256]{2,1,0:T(1,128)S(1)} %bitcast.62), channel_id=1, replica_groups=mesh['ctx'=32,'fsdp'=16] {'ctx'}, dimensions={0}, use_global_device_ids=true | all-gather | bytes 33792 | tf_op jit(solution)/shard_map/all_gather | solution.py:65
  475.4 3.7 all-gather.14.cloned.1.call-done
  479.1 7.7 fusion.9
  486.7 7.2 fusion.31
  493.9 108.1 %all-gather.16.cloned.1.call-done = bf16[8192,128]{0,1:T(8,128)(2,1)} async-done(((bf16[256,128]{0,1:T(8,128)(2,1)}), bf16[8192,128]{0,1:T(8,128)(2,1)}) %all-gather.16.cloned.1.call-update) | async-done | bytes 2097168 | tf_op jit(solution)/shard_map/all_gather | solution.py:62
  602.0 4.7 fusion.32
  606.8 7.1 fusion.35
  613.8 2.7 fusion.13
  616.5 4.5 fusion.14
  621.0 90.1 %reduce-scatter.2.cloned.1.call-done = bf16[256,384]{0,1:T(8,128)(2,1)} async-done(((bf16[4096,384]{0,1:T(8,128)(2,1)}), bf16[256,384]{0,1:T(8,128)(2,1)}) %reduce-scatter.2.cloned.1.call-update) | async-done | bytes 196624 | tf_op jit(solution)/shard_map/reduce_scatter | solution.py:83
  711.2 126.0 %all-reduce.1 = f32[256,384]{0,1:T(8,128)S(1)} all-reduce(bf16[256,384]{0,1:T(8,128)(2,1)} %reduce-scatter.2.cloned.1.call-done), channel_id=1, replica_groups=mesh['ctx'=32,'fsdp'=16] {'ctx'}, use_global_device_ids=true, to_apply=%region_7.8 | all-reduce | flops 98304 | bytes 589824 | tf_op jit(solution)/shard_map/psum | solution.py:89
  837.2 0.9 copy.21
  (27 shorter events, 2.1 us)
Async XLA Ops:
  7.2 76.0 %copy-start = (bf16[1,256,4096]{2,1,0:T(8,128)(2,1)S(1)}, bf16[1,256,4096]{2,1,0:T(8,128)(2,1)}, u32[]{:S(2)}) copy-start(bf16[1,256,4096]{2,1,0:T(8,128)(2,1)} %param.4) | copy-start | bytes 6291460
  7.2 81.1 %copy-start.3 = (bf16[1,256,128]{2,1,0:T(8,128)(2,1)S(1)}, bf16[1,256,128]{2,1,0:T(8,128)(2,1)}, u32[]{:S(2)}) copy-start(bf16[1,256,128]{2,1,0:T(8,128)(2,1)} %param.6) | copy-start | bytes 196612
  7.2 82.0 %copy-start.4 = (s32[1,16]{1,0:T(1,128)S(1)}, s32[1,16]{1,0:T(1,128)}, u32[]{:S(2)}) copy-start(s32[1,16]{1,0:T(1,128)} %param.5) | copy-start | bytes 196
  7.2 75.9 %all-gather.8.cloned.1.call-start = ((), (), s32[]{:S(2)}) async-start(), calls=%async_computation.1 | async-start | bytes 3342336 | tf_op jit(solution)/shard_map/all_gather | solution.py:34
  7.9 212.0 %all-gather.10.cloned.1.call-start = ((), (), s32[]{:S(2)}) async-start(), calls=%async_computation.2 | async-start | bytes 2162688 | tf_op jit(solution)/shard_map/all_gather | solution.py:41
  87.0 262.6 %all-gather.12.cloned.1.call-start = ((), (), s32[]{:S(2)}) async-start(), calls=%async_computation.3 | async-start | bytes 2162688 | tf_op jit(solution)/shard_map/all_gather | solution.py:42
  87.7 391.4 %all-gather.14.cloned.1.call-start = ((), (), s32[]{:S(2)}) async-start(), calls=%async_computation.4 | async-start | bytes 2162688 | tf_op jit(solution)/shard_map/all_gather | solution.py:59
  88.3 513.8 %all-gather.16.cloned.1.call-start = ((), (), s32[]{:S(2)}) async-start(), calls=%async_computation.5 | async-start | bytes 2162688 | tf_op jit(solution)/shard_map/all_gather | solution.py:62
  89.1 622.1 %reduce-scatter.2.cloned.1.call-start = ((), (), s32[]{:S(2)}) async-start(), calls=%async_computation.6 | async-start | bytes 3342336 | tf_op jit(solution)/shard_map/reduce_scatter | solution.py:83
  223.2 3.2 copy-start.1
  223.2 126.4 %copy-start.2 = (bf16[1,256,128]{1,2,0:T(8,128)(2,1)S(1)}, bf16[1,256,128]{1,2,0:T(8,128)(2,1)}, u32[]{:S(2)}) copy-start(bf16[1,256,128]{1,2,0:T(8,128)(2,1)} %copy.18) | copy-start | bytes 196612
Sparse Core Ops, SparseCore 0:
  11.3 71.7 all-gather.7
  87.1 132.7 all-gather.9
  222.6 126.9 all-gather.11
  352.1 126.9 all-gather.13
  480.9 121.0 all-gather.15
  616.6 94.4 reduce-scatter.1
where the time goes:
time: 846 us; the launch traced here: 845 us
  waiting for transfers between devices  532 us (63%)
  blocking collectives  246 us (29%)
  matrix products  45.9 us (5%)
  between operations  14.2 us (2%)
    all_gather x1, waiting for transfers between devices, local(): lax.all_gather(keys_own, 'ctx', axis=0, tiled=True)  130 us
    psum x1, blocking collectives, local(): grad_weights = lax.psum(block_sum, 'ctx')  126 us
    all_gather x1, waiting for transfers between devices, local(): lax.all_gather(values_own, 'ctx', axis=0, tiled=True)  123 us
    all_gather x1, waiting for transfers between devices, local(): lax.all_gather(grad_out.astype(jnp.float32), 'ctx', axis=0, tiled=True)  108 us
    reduce_scatter x1, waiting for transfers between devices, local(): lax.psum_scatter(lax.optimization_barrier(block_term).astype(jnp.float32)...  90.1 us
    all_gather x1, waiting for transfers between devices, local(): weights_all = lax.all_gather(w_qkv, 'fsdp', axis=0, tiled=True)  75.1 us
    all_gather x1, blocking collectives, local(): dot_piece = lax.all_gather(out_dot, 'ctx', axis=0, tiled=True)  61.5 us
    all_gather x1, blocking collectives, local(): total_piece = lax.all_gather(log_total, 'ctx', axis=0, tiled=True)  58.6 us
  transfers between devices with their start and end apart: 6, of which 6 were waited for; matrix products, arithmetic and copies ran while one was open for 4% of the time, Pallas kernels for 0%

commit v1 on v0

v1 whole, which is shorter than its diff:
```python
import functools

import jax
import jax.numpy as jnp
from jax import lax
from jax.experimental import pallas as pl
from jax.experimental.pallas import tpu as pltpu
from jax.sharding import PartitionSpec as P

MESH = pl.DeviceIdType.MESH
F32, BF16 = jnp.float32, jnp.bfloat16
NX, NYH, NC, NYL, NZ = 4, 2, 2, 2, 16
TOK, HD, D = 256, 128, 4096
QKV = 3 * HD
ROWS = D // (NX * NYH * NC)
NEG = -1e30
SCALE = HD ** -0.5
REACH = 5
HALF = TOK // 2
PAGES = 16


def fsdp_id(x, yh, core):
    return (x * NYH + yh) * NC + core


def ctx_id(yl, z):
    return yl * NZ + z


def place():
    ctx, f = lax.axis_index("ctx"), lax.axis_index("fsdp")
    return ctx // NZ, ctx % NZ, f // (NYH * NC), (f // NC) % NYH, f % NC


def rcopy(src, dst, send, recv, dev):
    return pltpu.make_async_remote_copy(
        src_ref=src, dst_ref=dst, send_sem=send, recv_sem=recv, device_id=dev, device_id_type=MESH
    )


def greet(peers):
    barrier = pltpu.get_barrier_semaphore()
    for dev in peers:
        pl.semaphore_signal(barrier, inc=1, device_id=dev, device_id_type=MESH)
    pl.semaphore_wait(barrier, len(peers))


def nt(a, b):
    return lax.dot_general(a, b, (((1,), (1,)), ((), ())), preferred_element_type=F32)


def tn(a, b):
    return lax.dot_general(a, b, (((0,), (0,)), ((), ())), preferred_element_type=F32)


def nn(a, b):
    return jnp.dot(a, b, preferred_element_type=F32)


def neighbours():
    yl, z, x, yh, core = place()
    ctx, f = ctx_id(yl, z), fsdp_id(x, yh, core)
    left, right = (x + NX - 1) % NX, (x + 1) % NX
    dev_l, dev_r = (ctx, fsdp_id(left, yh, core)), (ctx, fsdp_id(right, yh, core))
    dev_y = (ctx_id(1 - yl, z), fsdp_id(x, 1 - yh, core))
    dev_s = (ctx, fsdp_id(x, yh, 1 - core))
    return dev_l, dev_r, dev_y, dev_s


def gather_kernel(
    hid_hbm, w_hbm, do_hbm, wall_out, proj_out, doall, pdo,
    hid, wall, wsend, wrecv, dsend, drecv, loc,
):
    yl, z, x, yh, core = place()
    ctx, f = ctx_id(yl, z), fsdp_id(x, yh, core)
    left, right, far = (x + NX - 1) % NX, (x + 1) % NX, (x + 2) % NX
    dev_l, dev_r, dev_y, dev_s = neighbours()
    dev_p = (ctx_id(1 - yl, z), f)
    dev_zl, dev_zr = (ctx_id(yl, (z + NZ - 1) % NZ), f), (ctx_id(yl, (z + 1) % NZ), f)
    greet([dev_l, dev_r, dev_y, dev_s, dev_p, dev_zl, dev_zr])

    hid_copy = pltpu.make_async_copy(hid_hbm, hid, loc.at[0])
    own_copy = pltpu.make_async_copy(w_hbm, wall.at[f], loc.at[1])
    do_copy = pltpu.make_async_copy(do_hbm, doall.at[z], loc.at[2])
    sent = []

    def send(src, dst, slot, dev):
        copy = rcopy(src, dst, wsend.at[len(sent)], wrecv.at[slot], dev)
        copy.start()
        sent.append(copy)

    def arrived(ref, slot):
        rcopy(ref, ref, wsend.at[0], wrecv.at[slot], dev_s).wait_recv()

    lo, hi = pl.ds(0, HALF), pl.ds(HALF, HALF)
    for slot, dev in ((1, dev_r), (2, dev_l), (0, dev_y), (9, dev_s)):
        send(w_hbm, wall.at[f], slot, dev)
    own_copy.start()
    do_copy.start()
    hid_copy.start()
    dsent = []

    def dsendto(src, dst, slot, dev):
        copy = rcopy(src, dst, dsend.at[len(dsent)], drecv.at[slot], dev)
        copy.start()
        dsent.append(copy)

    dsendto(do_hbm, doall.at[z], 1, dev_zr)
    dsendto(do_hbm, doall.at[z], 9, dev_zl)
    dsendto(do_hbm, pdo, 0, dev_p)

    def do_step(d):
        zl, zr = (z + NZ - d) % NZ, (z + d) % NZ
        from_l, from_r = doall.at[zl], doall.at[zr]
        if d == NZ // 2:
            from_l, from_r = doall.at[zl, lo], doall.at[zr, hi]
        rcopy(from_l, from_l, dsend.at[0], drecv.at[d], dev_p).wait_recv()
        if d < NZ // 2:
            on = doall.at[zl, lo] if d == NZ // 2 - 1 else from_l
            dsendto(on, on, d + 1, dev_zr)
        rcopy(from_r, from_r, dsend.at[0], drecv.at[8 + d], dev_p).wait_recv()
        if d < NZ // 2:
            on = doall.at[zr, hi] if d == NZ // 2 - 1 else from_r
            dsendto(on, on, 9 + d, dev_zl)

    def own(xx, yy):
        return fsdp_id(xx, yy, core)

    def sib(xx, yy):
        return fsdp_id(xx, yy, 1 - core)

    yc = 1 - yh
    c = wall.at[own(x, yc)]
    arrived(c, 0)
    send(c, c, 3, dev_r)
    send(c, c, 4, dev_l)
    send(c, c, 10, dev_s)
    ol, orr = wall.at[own(left, yh)], wall.at[own(right, yh)]
    arrived(ol, 1)
    on = wall.at[own(left, yh), lo]
    send(on, on, 5, dev_r)
    send(ol, ol, 11, dev_s)
    arrived(orr, 2)
    on = wall.at[own(right, yh), hi]
    send(on, on, 6, dev_l)
    send(orr, orr, 12, dev_s)
    do_step(1)
    fa, fb = wall.at[own(far, yh), lo], wall.at[own(far, yh), hi]
    arrived(fa, 5)
    send(fa, fa, 7, dev_y)
    send(fa, fa, 15, dev_s)
    arrived(fb, 6)
    send(fb, fb, 8, dev_y)
    send(fb, fb, 16, dev_s)
    do_step(2)
    cl, cr = wall.at[own(left, yc)], wall.at[own(right, yc)]
    arrived(cl, 3)
    send(cl, cl, 13, dev_s)
    arrived(cr, 4)
    send(cr, cr, 14, dev_s)
    do_step(3)
    ca, cb = wall.at[own(far, yc), lo], wall.at[own(far, yc), hi]
    arrived(ca, 7)
    send(ca, ca, 17, dev_s)
    arrived(cb, 8)
    send(cb, cb, 18, dev_s)
    do_step(4)
    for slot, ref in (
        (9, wall.at[sib(x, yh)]), (10, wall.at[sib(x, yc)]), (11, wall.at[sib(left, yh)]),
        (12, wall.at[sib(right, yh)]), (13, wall.at[sib(left, yc)]), (14, wall.at[sib(right, yc)]),
        (15, wall.at[sib(far, yh), lo]), (16, wall.at[sib(far, yh), hi]),
        (17, wall.at[sib(far, yc), lo]), (18, wall.at[sib(far, yc), hi]),
    ):
        arrived(ref, slot)
    own_copy.wait()
    wall_copy = pltpu.make_async_copy(wall, wall_out, loc.at[1])
    wall_copy.start()
    hid_copy.wait()
    total = jnp.zeros((TOK, QKV), F32)
    for s in range(NX * NYH * NC):
        if s in (0, 5, 10):
            do_step(5 + s // 5)
        total += nn(hid[:, s * ROWS : (s + 1) * ROWS], wall[s])
    proj_out[...] = total.astype(BF16)
    do_step(8)
    rcopy(pdo, pdo, dsend.at[0], drecv.at[0], dev_p).wait_recv()
    for copy in sent + dsent:
        copy.wait_send()
    do_copy.wait()
    wall_copy.wait()


def gather_weights(hidden, w, grad_out):
    n = NX * NYH * NC
    any_spec = pl.BlockSpec(memory_space=pl.ANY)
    vmem = pl.BlockSpec(memory_space=pltpu.VMEM)
    return pl.pallas_call(
        gather_kernel,
        out_shape=(
            jax.ShapeDtypeStruct((n, ROWS, QKV), BF16),
            jax.ShapeDtypeStruct((TOK, QKV), BF16),
            jax.ShapeDtypeStruct((NZ, TOK, HD), BF16),
            jax.ShapeDtypeStruct((TOK, HD), BF16),
        ),
        in_specs=[any_spec] * 3,
        out_specs=(any_spec, vmem, vmem, vmem),
        scratch_shapes=[
            pltpu.VMEM((TOK, D), BF16),
            pltpu.VMEM((n, ROWS, QKV), BF16),
            pltpu.SemaphoreType.DMA((19,)),
            pltpu.SemaphoreType.DMA((19,)),
            pltpu.SemaphoreType.DMA((17,)),
            pltpu.SemaphoreType.DMA((17,)),
            pltpu.SemaphoreType.DMA((3,)),
        ],
        compiler_params=pltpu.CompilerParams(
            collective_id=0, has_side_effects=True, vmem_limit_bytes=24 << 20
        ),
        name="gather_weights",
    )(hidden, w, grad_out)


def attend_kernel(
    pages, proj, doall, pdo, grad_qkv,
    qkv, pqkv, q2, do2, lim_q, lim_col, s_keep, dp_keep, mlu, mlu_in, stats, dqt, dkv, out_x, in_x, out_kv, in_kv,
    zsend, zrecv, psend, precv, ssend, srecv,
):
    yl, z, x, yh, core = place()
    f = fsdp_id(x, yh, core)
    dev_p = (ctx_id(1 - yl, z), f)

    def at_z(d):
        return (ctx_id(yl, (z + d) % NZ), f)

    dev_zl, dev_zr = at_z(NZ - 1), at_z(1)
    greet([dev_p] + [at_z(d) for d in range(1, NZ)])
    lo, hi = pl.ds(0, HALF), pl.ds(HALF, HALF)

    first = [
        rcopy(proj, qkv.at[z], zsend.at[0, 0], zrecv.at[0, 1], dev_zr),
        rcopy(proj, qkv.at[z], zsend.at[1, 0], zrecv.at[1, 1], dev_zl),
        rcopy(proj, pqkv, psend.at[0], precv.at[0], dev_p),
    ]
    for copy in first:
        copy.start()
    qkv[z] = proj[...]

    ends = []
    total = 0
    for page in range(PAGES):
        total = total + pages[0, page]
        ends.append(total)

    def limits(pos):
        out = jnp.full(pos.shape, NYL * NZ * TOK, jnp.int32)
        for end in ends:
            out = jnp.minimum(out, jnp.where(pos < end, end, NYL * NZ * TOK))
        return out

    lane = lax.broadcasted_iota(jnp.int32, (1, TOK), 1)
    lim_q[:, :TOK] = limits(ctx_id(yl, z) * TOK + lane)
    lim_q[:, TOK:] = limits(ctx_id(1 - yl, z) * TOK + lane)

    @pl.loop(0, NZ)
    def _(j):
        lim_col[j] = limits(ctx_id(yl, j) * TOK + lane)

    q2[:TOK] = proj[:, :HD]
    do2[:TOK] = doall[z]
    do2[TOK:] = pdo[...]
    mlu[0:1] = jnp.full((1, 2 * TOK), NEG, F32)
    mlu[1:8] = jnp.zeros((7, 2 * TOK), F32)
    first[2].wait_recv()
    q2[TOK:] = pqkv[:, :HD]

    key_row = lax.broadcasted_iota(jnp.int32, (TOK, 1), 0)

    def score_block(j):
        s = nt(qkv[j, :, HD : 2 * HD], q2[...]) * SCALE
        dp = nt(qkv[j, :, 2 * HD :], do2[...])
        s = jnp.where(ctx_id(yl, j) * TOK + key_row < lim_q[...], s, NEG)
        s_keep[j] = s
        dp_keep[j] = dp
        m = mlu[0:1]
        m_new = jnp.maximum(m, jnp.max(s, axis=0, keepdims=True))
        p = jnp.exp(s - m_new)
        a = jnp.exp(m - m_new)
        mlu[0:1] = m_new
        mlu[1:2] = mlu[1:2] * a + jnp.sum(p, axis=0, keepdims=True)
        mlu[2:3] = mlu[2:3] * a + jnp.sum(p * dp, axis=0, keepdims=True)

    last_q = ctx_id(1, z)

    def score(j):
        @pl.when(ctx_id(yl, j) <= last_q + REACH)
        def _():
            score_block(j)

    score(z)

    def passed(d):
        zl, zr = (z + NZ - d) % NZ, (z + d) % NZ
        rcopy(qkv.at[zl], qkv.at[zl], zsend.at[0, d], zrecv.at[0, d], dev_zr).wait_recv()
        return zl, zr

    @pl.loop(1, NZ // 2 - 1)
    def _(d):
        zl, zr = passed(d)
        rcopy(qkv.at[zl], qkv.at[zl], zsend.at[0, d], zrecv.at[0, d + 1], dev_zr).start()
        rcopy(qkv.at[zr], qkv.at[zr], zsend.at[1, d], zrecv.at[1, d], dev_zl).wait_recv()
        rcopy(qkv.at[zr], qkv.at[zr], zsend.at[1, d], zrecv.at[1, d + 1], dev_zl).start()

        @pl.loop(0, 2)
        def _(side):
            score((z + NZ - d + 2 * d * side) % NZ)

    d = NZ // 2 - 1
    zl, zr = passed(d)
    on = qkv.at[zl, lo]
    tail_r = rcopy(on, on, zsend.at[0, d], zrecv.at[0, d + 1], dev_zr)
    tail_r.start()
    rcopy(qkv.at[zr], qkv.at[zr], zsend.at[1, d], zrecv.at[1, d], dev_zl).wait_recv()
    on = qkv.at[zr, hi]
    tail_l = rcopy(on, on, zsend.at[1, d], zrecv.at[1, d + 1], dev_zl)
    tail_l.start()
    score(zl)
    score(zr)
    opp = (z + NZ // 2) % NZ
    rcopy(qkv.at[opp, lo], qkv.at[opp, lo], zsend.at[0, 0], zrecv.at[0, d + 1], dev_zr).wait_recv()
    rcopy(qkv.at[opp, hi], qkv.at[opp, hi], zsend.at[1, 0], zrecv.at[1, d + 1], dev_zl).wait_recv()
    score(opp)

    trade = rcopy(mlu, mlu_in, psend.at[1], precv.at[1], dev_p)
    trade.start()
    trade.wait_recv()

    def merge(mine, theirs):
        m1, m2 = mlu[0:1, mine], mlu_in[0:1, theirs]
        m = jnp.maximum(m1, m2)
        a1, a2 = jnp.exp(m1 - m), jnp.exp(m2 - m)
        l = mlu[1:2, mine] * a1 + mlu_in[1:2, theirs] * a2
        u = mlu[2:3, mine] * a1 + mlu_in[2:3, theirs] * a2
        return m + jnp.log(l), u / l

    own_q, par_q = slice(0, TOK), slice(TOK, 2 * TOK)
    lse_own, dot_own = merge(own_q, par_q)
    lse_par, dot_par = merge(par_q, own_q)
    stats[z, 0:1] = lse_own
    stats[z, 1:2] = dot_own
    stats[z, 2:8] = jnp.zeros((6, TOK), F32)

    @pl.loop(1, NZ)
    def _(d):
        rcopy(stats.at[z], stats.at[z], ssend.at[d], srecv.at[d], at_z(d)).start()

    trade.wait_send()
    mlu[0:1] = jnp.concatenate([lse_own, lse_par], axis=1)
    mlu[1:2] = jnp.concatenate([dot_own, dot_par], axis=1)
    dqt[...] = jnp.zeros((HD, 2 * TOK), F32)

    @pl.loop(0, NZ)
    def _(j):
        @pl.when(ctx_id(yl, j) <= last_q + REACH)
        def _():
            p = jnp.exp(s_keep[j] - mlu[0:1])
            ds = (p * (dp_keep[j] - mlu[1:2]) * SCALE).astype(BF16)
            dqt[...] += tn(qkv[j, :, HD : 2 * HD], ds)

    out_x[...] = dqt[:, TOK:].astype(BF16)
    dq_copy = rcopy(out_x, in_x, psend.at[2], precv.at[2], dev_p)
    dq_copy.start()

    def key_block(src, k_block, j):
        s = nt(src[:, HD : 2 * HD], qkv[j, :, :HD]) * SCALE
        dp = nt(src[:, 2 * HD :], doall[j])
        s = jnp.where(k_block * TOK + key_row < lim_col[j], s, NEG)
        p = jnp.exp(s - stats[j, 0:1])
        ds = (p * (dp - stats[j, 1:2]) * SCALE).astype(BF16)
        dkv[:, :HD] += nn(ds, qkv[j, :, :HD])
        dkv[:, HD:] += nn(p.astype(BF16), doall[j])

    def keys(src, k_block, wait):
        dkv[...] = jnp.zeros((TOK, 2 * HD), F32)

        @pl.loop(0, NZ)
        def _(d):
            j = (z + NZ - d) % NZ
            if wait:
                @pl.when(d > 0)
                def _():
                    rcopy(stats.at[j], stats.at[j], ssend.at[d], srecv.at[d], dev_p).wait_recv()

            @pl.when(k_block <= ctx_id(yl, j) + REACH)
            def _():
                key_block(src, k_block, j)

    keys(pqkv, ctx_id(1 - yl, z), True)
    out_kv[...] = dkv[...].astype(BF16)
    kv_copy = rcopy(out_kv, in_kv, psend.at[3], precv.at[3], dev_p)
    kv_copy.start()
    keys(proj, ctx_id(yl, z), False)
    dq_copy.wait_recv()
    grad_qkv[:, :HD] = (dqt[:, :TOK] + in_x[...].astype(F32)).T.astype(BF16)
    kv_copy.wait_recv()
    grad_qkv[:, HD:] = (dkv[...] + in_kv[...].astype(F32)).astype(BF16)

    for copy in first:
        copy.wait_send()

    @pl.loop(1, NZ // 2 - 1)
    def _(d):
        rcopy(proj, proj, zsend.at[0, d], zrecv.at[0, d], dev_zr).wait_send()
        rcopy(proj, proj, zsend.at[1, d], zrecv.at[1, d], dev_zl).wait_send()

    tail_r.wait_send()
    tail_l.wait_send()
    dq_copy.wait_send()
    kv_copy.wait_send()

    @pl.loop(1, NZ)
    def _(d):
        rcopy(stats.at[z], stats.at[z], ssend.at[d], srecv.at[d], dev_p).wait_send()


def attend(pages, proj, doall, pdo):
    vmem = pl.BlockSpec(memory_space=pltpu.VMEM)
    dma = pltpu.SemaphoreType.DMA
    return pl.pallas_call(
        attend_kernel,
        out_shape=jax.ShapeDtypeStruct((TOK, QKV), BF16),
        in_specs=[pl.BlockSpec(memory_space=pltpu.SMEM), vmem, vmem, vmem],
        out_specs=vmem,
        scratch_shapes=[
            pltpu.VMEM((NZ, TOK, QKV), BF16),
            pltpu.VMEM((TOK, QKV), BF16),
            pltpu.VMEM((2 * TOK, HD), BF16),
            pltpu.VMEM((2 * TOK, HD), BF16),
            pltpu.VMEM((1, 2 * TOK), jnp.int32),
            pltpu.VMEM((NZ, 1, TOK), jnp.int32),
            pltpu.VMEM((NZ, TOK, 2 * TOK), F32),
            pltpu.VMEM((NZ, TOK, 2 * TOK), F32),
            pltpu.VMEM((8, 2 * TOK), F32),
            pltpu.VMEM((8, 2 * TOK), F32),
            pltpu.VMEM((NZ, 8, TOK), F32),
            pltpu.VMEM((HD, 2 * TOK), F32),
            pltpu.VMEM((TOK, 2 * HD), F32),
            pltpu.VMEM((HD, TOK), BF16),
            pltpu.VMEM((HD, TOK), BF16),
            pltpu.VMEM((TOK, 2 * HD), BF16),
            pltpu.VMEM((TOK, 2 * HD), BF16),
            dma((2, NZ // 2)),
            dma((2, NZ // 2 + 1)),
            dma((4,)),
            dma((4,)),
            dma((NZ,)),
            dma((NZ,)),
        ],
        compiler_params=pltpu.CompilerParams(
            collective_id=1, has_side_effects=True, vmem_limit_bytes=40 << 20
        ),
        name="attend",
    )(pages, proj, doall, pdo)


PATCH = 8
SLICE = ROWS // PATCH


def reduce_kernel(
    hid_hbm, gq, gw_out,
    hid, term, sib, sib_in, got, gotb, relay, total, part, part_in, mid, mid_in, fin, loc, csend, crecv, nsend, nrecv, asend, arecv,
):
    yl, z, x, yh, core = place()
    ctx, f = ctx_id(yl, z), fsdp_id(x, yh, core)
    dev_l, dev_r, dev_y, dev_s = neighbours()
    zl, zh = z % 4, z // 4

    def patch_dev(i):
        return (ctx_id(i // 4, zh * 4 + i % 4), f)

    me = yl * 4 + zl
    peers = [(me + i) % PATCH for i in range(1, PATCH)]
    far_z = [(ctx_id(yl, (z + 4 * i) % NZ), f) for i in range(1, 4)]
    hid_copy = pltpu.make_async_copy(hid_hbm, hid, loc.at[0])
    hid_copy.start()
    greet([dev_l, dev_r, dev_y, dev_s] + [patch_dev(i) for i in peers] + far_z)
    hid_copy.wait()

    n8 = NX * NYH
    lo, hi = pl.ds(0, HALF), pl.ds(HALF, HALF)

    def block(s):
        return tn(hid[:, pl.ds(pl.multiple_of(s * ROWS, ROWS), ROWS)], gq[...])

    @pl.loop(0, n8)
    def _(i):
        sib[i] = block(2 * i + 1 - core).astype(BF16)
        rcopy(sib.at[i], sib_in.at[i], csend.at[i], crecv.at[i], dev_s).start()

    @pl.loop(0, n8)
    def _(i):
        mine = block(2 * i + core)
        rcopy(sib_in.at[i], sib_in.at[i], csend.at[i], crecv.at[i], dev_s).wait_recv()
        term[i] = (mine + sib_in[i].astype(F32)).astype(BF16)

    left, right, far = (x + NX - 1) % NX, (x + 1) % NX, (x + 2) % NX
    yc = 1 - yh

    def at(xx, yy):
        return xx * NYH + yy

    sent = []

    def send(src, dst, slot, dev):
        copy = rcopy(src, dst, nsend.at[len(sent)], nrecv.at[slot], dev)
        copy.start()
        sent.append(copy)

    def arrived(ref, slot):
        rcopy(ref, ref, nsend.at[0], nrecv.at[slot], dev_s).wait_recv()

    send(term.at[at(far, yc)], got.at[0], 0, dev_y)
    send(term.at[at(left, yc)], got.at[2], 2, dev_l)
    send(term.at[at(right, yc)], got.at[1], 1, dev_r)
    arrived(got.at[0], 0)
    relay[0] = (term[at(far, yh)].astype(F32) + got[0].astype(F32)).astype(BF16)
    send(relay.at[0, lo], gotb.at[0], 6, dev_r)
    send(relay.at[0, hi], gotb.at[1], 7, dev_l)
    arrived(got.at[1], 1)
    arrived(got.at[2], 2)
    relay[1] = (term[at(x, yc)].astype(F32) + got[1].astype(F32) + got[2].astype(F32)).astype(BF16)
    send(relay.at[1], got.at[5], 5, dev_y)
    arrived(gotb.at[0], 6)
    relay[2, :HALF] = (term[at(right, yh), :HALF].astype(F32) + gotb[0].astype(F32)).astype(BF16)
    relay[2, HALF:] = term[at(right, yh), HALF:]
    send(relay.at[2], got.at[3], 3, dev_r)
    arrived(gotb.at[1], 7)
    relay[3, HALF:] = (term[at(left, yh), HALF:].astype(F32) + gotb[1].astype(F32)).astype(BF16)
    relay[3, :HALF] = term[at(left, yh), :HALF]
    send(relay.at[3], got.at[4], 4, dev_l)
    arrived(got.at[5], 5)
    arrived(got.at[3], 3)
    arrived(got.at[4], 4)
    total[...] = (
        term[at(x, yh)].astype(F32) + got[3].astype(F32) + got[4].astype(F32) + got[5].astype(F32)
    )
    part[...] = total[...].astype(BF16).reshape(PATCH, SLICE, QKV)

    for i in range(1, PATCH):
        to = (me + i) % PATCH
        copy = rcopy(part.at[to], part_in.at[i], asend.at[i], arecv.at[i], patch_dev(to))
        copy.start()
        sent.append(copy)
    acc = total[pl.ds(pl.multiple_of(me * SLICE, SLICE), SLICE), :]
    for i in range(1, PATCH):
        rcopy(part_in.at[i], part_in.at[i], asend.at[i], arecv.at[i], dev_s).wait_recv()
        acc += part_in[i].astype(F32)
    mid[...] = acc.astype(BF16)
    for i in range(1, 4):
        copy = rcopy(mid, mid_in.at[i], asend.at[7 + i], arecv.at[7 + i], far_z[i - 1])
        copy.start()
        sent.append(copy)
    for i in range(1, 4):
        rcopy(mid_in.at[i], mid_in.at[i], asend.at[7 + i], arecv.at[7 + i], dev_s).wait_recv()
    mid_in[0] = mid[...]
    acc = jnp.zeros((SLICE, QKV), F32)
    for h in range(4):
        acc += mid_in[(zh - h + 4) % 4].astype(F32)
    fin[me] = acc.astype(BF16)
    for i in range(1, PATCH):
        to = (me + i) % PATCH
        copy = rcopy(fin.at[me], fin.at[me], asend.at[10 + i], arecv.at[10 + i], patch_dev(to))
        copy.start()
        sent.append(copy)
    for i in range(1, PATCH):
        src = fin.at[(me + PATCH - i) % PATCH]
        rcopy(src, src, asend.at[10 + i], arecv.at[10 + i], dev_s).wait_recv()
    gw_out[...] = fin[...].reshape(ROWS, QKV).astype(F32)
    for copy in sent:
        copy.wait_send()

    @pl.loop(0, n8)
    def _(i):
        rcopy(sib.at[i], sib_in.at[i], csend.at[i], crecv.at[i], dev_s).wait_send()


def reduce_weights(hidden, gq):
    n8 = NX * NYH
    vmem = pl.BlockSpec(memory_space=pltpu.VMEM)
    dma = pltpu.SemaphoreType.DMA
    return pl.pallas_call(
        reduce_kernel,
        out_shape=jax.ShapeDtypeStruct((ROWS, QKV), F32),
        in_specs=[pl.BlockSpec(memory_space=pl.ANY), vmem],
        out_specs=vmem,
        scratch_shapes=[
            pltpu.VMEM((TOK, D), BF16),
            pltpu.VMEM((n8, ROWS, QKV), BF16),
            pltpu.VMEM((n8, ROWS, QKV), BF16),
            pltpu.VMEM((n8, ROWS, QKV), BF16),
            pltpu.VMEM((6, ROWS, QKV), BF16),
            pltpu.VMEM((2, HALF, QKV), BF16),
            pltpu.VMEM((4, ROWS, QKV), BF16),
            pltpu.VMEM((ROWS, QKV), F32),
            pltpu.VMEM((PATCH, SLICE, QKV), BF16),
            pltpu.VMEM((PATCH, SLICE, QKV), BF16),
            pltpu.VMEM((SLICE, QKV), BF16),
            pltpu.VMEM((4, SLICE, QKV), BF16),
            pltpu.VMEM((PATCH, SLICE, QKV), BF16),
            dma((1,)),
            dma((n8,)),
            dma((n8,)),
            dma((8,)),
            dma((8,)),
            dma((18,)),
            dma((18,)),
        ],
        compiler_params=pltpu.CompilerParams(
            collective_id=2, has_side_effects=True, vmem_limit_bytes=32 << 20
        ),
        name="reduce_weights",
    )(hidden, gq)


def local(hidden_in, page_tokens, grad_attn, w_qkv):
    hidden = hidden_in[0]
    wall, proj, doall, pdo = gather_weights(hidden, w_qkv, grad_attn[0])
    gq = attend(page_tokens, proj, doall, pdo)
    grad_w = reduce_weights(hidden, gq)
    grad_hidden = nt(gq, wall.reshape(D, QKV)).astype(BF16)[None]
    return grad_hidden, grad_w


def solution(mesh):
    in_specs = (P("fsdp", "ctx", None), P("fsdp", None), P("fsdp", "ctx", None), P("fsdp", None))
    out_specs = (P("fsdp", "ctx", None), P("fsdp", None))
    return jax.shard_map(local, mesh=mesh, in_specs=in_specs, out_specs=out_specs, check_vma=False)
```

time: 846 us -> 179 us (0.21)
  waiting for transfers between devices: 532 us -> 0 us
  blocking collectives: 246 us -> 0 us
  Pallas kernels: 0 us -> 171 us
  matrix products: 45.9 us -> 2.61 us
  between operations: 14.2 us -> 0.67 us
    all_gather x5 -> x0, waiting for transfers between devices: 440 us -> none  [the longest x1 130 us: local(): lax.all_gather(keys_own, 'ctx', axis=0, tiled=True)]
    pallas_call x0 -> x3, Pallas kernels: none -> 171 us  [the longest x1 73.8 us: attend(): pl.pallas_call(attend_kernel, out_shape=jax.ShapeDtypeStruct((TOK, QKV),...]
    psum x1 -> x0, blocking collectives: 126 us -> none  [local(): grad_weights = lax.psum(block_sum, 'ctx')]
    all_gather x2 -> x0, blocking collectives: 120 us -> none  [the longest x1 61.5 us: local(): dot_piece = lax.all_gather(out_dot, 'ctx', axis=0, tiled=True)]
    reduce_scatter x1 -> x0, waiting for transfers between devices: 90.1 us -> none  [local(): lax.psum_scatter(lax.optimization_barrier(block_term).astype(jnp.float32)...]
    dot_general x9 -> x1, matrix products: 45.9 us -> 2.61 us  [nt(): lax.dot_general(a, b, (((1,), (1,)), ((), ())), preferred_element_type=F32)]
  transfers between devices with their start and end apart: 6 -> 0, of which waited for: 6 -> 0; matrix products, arithmetic and copies ran while one was open for 4% -> 0% of each run, Pallas kernels for 0% -> 0%
where the time goes in v1:
time: 179 us
  Pallas kernels  171 us (96%)
  local copies, waits for them, and re-layouts  4.75 us (3%)
  matrix products  2.61 us (1%)
    pallas_call x1, Pallas kernels, attend(): pl.pallas_call(attend_kernel, out_shape=jax.ShapeDtypeStruct((TOK, QKV),...  73.8 us
    pallas_call x1, Pallas kernels, reduce_weights(): pl.pallas_call(reduce_kernel, out_shape=jax.ShapeDtypeStruct((ROWS, QKV),...  48.6 us
    pallas_call x1, Pallas kernels, gather_weights(): pl.pallas_call(gather_kernel, out_shape=(jax.ShapeDtypeStruct((n, ROWS, Q...  48.5 us
    unnamed x11, local copies, waits for them, and re-layouts  4.75 us

profile of v1, /device:TPU:6, one launch (start us, length us, event | category | flops | bytes accessed | tf_op | source)
XLA Modules:
  0.0 178.9 jit_solution(15996178029603670682)
XLA Ops:
  0.6 0.0 copy-start
  0.6 1.6 copy-done
  2.2 0.0 copy-start.2
  2.2 0.9 copy-done.2
  3.2 0.0 copy-start.3
  3.2 0.8 copy-done.3
  4.0 48.5 %gather_weights.1 = (bf16[16,256,384]{2,1,0:T(8,128)(2,1)S(1)}, bf16[256,384]{1,0:T(8,128)(2,1)S(1)}, bf16[16,256,128]{2,1,0:T(8,128)(2,1)S(1)}, bf16[256,128]{1,0:T(8,128)(2,1)S(1)}) custom-call(bf16[256,4096]{1,0:T(8,128)(2,1)S(1)} %bitcast.7, bf16[256,384]{1,0:T(8,128)(2,1)S(1)} %copy-done.2, bf16[256,128]{1,0:T(8,128)(2,1)S(1)} %bitcast.10), custom_call_target="tpu_custom_call" | custom-call | tf_op jit(solution)/shard_map/gather_weights/pallas_call | solution.py:198
  52.5 0.0 copy-start.4
  52.5 0.6 copy-done.4
  53.1 0.0 copy-start.1
  53.1 73.8 %attend.1.gq = bf16[256,384]{1,0:T(8,128)(2,1)S(1)} custom-call(s32[1,16]{1,0:T(1,128)S(1)} %copy-done.4, bf16[256,384]{1,0:T(8,128)(2,1)S(1)} %get-tuple-element.6.proj, bf16[16,256,128]{2,1,0:T(8,128)(2,1)S(1)} %get-tuple-element.7.doall, bf16[256,128]{1,0:T(8,128)(2,1)S(1)} %get-tuple-element.8.pdo), custom_call_target="tpu_custom_call" | custom-call | tf_op jit(solution)/shard_map/attend/pallas_call | solution.py:429
  126.9 2.6 %fusion = bf16[1,256,4096]{2,1,0:T(8,128)(2,1)} fusion(bf16[256,384]{1,0:T(8,128)(2,1)S(1)} %attend.1.gq, bf16[4096,384]{1,0:T(8,128)(2,1)S(1)} %bitcast.9), kind=kOutput, calls=%fused_computation.1 | convolution fusion | flops 806354944 | bytes 5439488 | tf_op jit(solution)/shard_map/dot_general | solution.py:50
  129.5 0.0 copy-done.1
  129.5 48.6 %reduce_weights.1 = f32[256,384]{1,0:T(8,128)S(1)} custom-call(bf16[256,4096]{1,0:T(8,128)(2,1)S(1)} %bitcast.8, bf16[256,384]{1,0:T(8,128)(2,1)S(1)} %attend.1.gq), custom_call_target="tpu_custom_call" | custom-call | tf_op jit(solution)/shard_map/reduce_weights/pallas_call | solution.py:592
  178.2 0.7 copy.7
Async XLA Ops:
  0.6 1.6 copy-start
  2.2 0.9 copy-start.2
  3.2 0.8 copy-start.3
  52.5 0.7 copy-start.4
  53.1 76.4 %copy-start.1 = (bf16[1,256,4096]{2,1,0:T(8,128)(2,1)S(1)}, bf16[1,256,4096]{2,1,0:T(8,128)(2,1)}, u32[]{:S(2)}) copy-start(bf16[1,256,4096]{2,1,0:T(8,128)(2,1)} %param.4) | copy-start | bytes 6291460

commit v2 on v1

v2 whole, which is shorter than its diff:
```python
import functools

import jax
import jax.numpy as jnp
from jax import lax
from jax.experimental import pallas as pl
from jax.experimental.pallas import tpu as pltpu
from jax.sharding import PartitionSpec as P

MESH = pl.DeviceIdType.MESH
F32, BF16 = jnp.float32, jnp.bfloat16
NX, NYH, NC, NYL, NZ = 4, 2, 2, 2, 16
TOK, HD, D = 256, 128, 4096
QKV = 3 * HD
ROWS = D // (NX * NYH * NC)
NEG = -1e30
SCALE = HD ** -0.5
REACH = 5
HALF = TOK // 2
PAGES = 16
LAG = 3


def fsdp_id(x, yh, core):
    return (x * NYH + yh) * NC + core


def ctx_id(yl, z):
    return yl * NZ + z


def place():
    ctx, f = lax.axis_index("ctx"), lax.axis_index("fsdp")
    return ctx // NZ, ctx % NZ, f // (NYH * NC), (f // NC) % NYH, f % NC


def rcopy(src, dst, send, recv, dev):
    return pltpu.make_async_remote_copy(
        src_ref=src, dst_ref=dst, send_sem=send, recv_sem=recv, device_id=dev, device_id_type=MESH
    )


def greet(peers):
    barrier = pltpu.get_barrier_semaphore()
    for dev in peers:
        pl.semaphore_signal(barrier, inc=1, device_id=dev, device_id_type=MESH)
    pl.semaphore_wait(barrier, len(peers))


def nt(a, b):
    return lax.dot_general(a, b, (((1,), (1,)), ((), ())), preferred_element_type=F32)


def tn(a, b):
    return lax.dot_general(a, b, (((0,), (0,)), ((), ())), preferred_element_type=F32)


def nn(a, b):
    return jnp.dot(a, b, preferred_element_type=F32)


def neighbours():
    yl, z, x, yh, core = place()
    ctx, f = ctx_id(yl, z), fsdp_id(x, yh, core)
    left, right = (x + NX - 1) % NX, (x + 1) % NX
    dev_l, dev_r = (ctx, fsdp_id(left, yh, core)), (ctx, fsdp_id(right, yh, core))
    dev_y = (ctx_id(1 - yl, z), fsdp_id(x, 1 - yh, core))
    dev_s = (ctx, fsdp_id(x, yh, 1 - core))
    return dev_l, dev_r, dev_y, dev_s


def front_kernel(
    pages, hid_hbm, w_hbm, do_hbm, wall_out, grad_qkv,
    hid, wall, acc, proj, pqkv, kall, vall, qall, doall, pdo, q2, do2, lim_q, lim_col, s_keep, dp_keep, mlu, mlu_in,
    stats, dqt, dkv, out_x, in_x, out_kv, in_kv, wsend, wrecv, zsend, zrecv, psend, precv, ssend, srecv, loc,
):
    yl, z, x, yh, core = place()
    ctx, f = ctx_id(yl, z), fsdp_id(x, yh, core)
    left, right, far = (x + NX - 1) % NX, (x + 1) % NX, (x + 2) % NX
    dev_l, dev_r, dev_y, dev_s = neighbours()
    dev_p = (ctx_id(1 - yl, z), f)

    def at_z(d):
        return (ctx_id(yl, (z + d) % NZ), f)

    dev_zl, dev_zr = at_z(NZ - 1), at_z(1)
    greet([dev_l, dev_r, dev_y, dev_s, dev_p, dev_zl, dev_zr])

    sent = []

    def send(src, dst, slot, dev):
        copy = rcopy(src, dst, wsend.at[len(sent)], wrecv.at[slot], dev)
        copy.start()
        sent.append(copy)

    def arrived(ref, slot):
        rcopy(ref, ref, wsend.at[0], wrecv.at[slot], dev_s).wait_recv()

    rings = ((kall, 8, 7), (vall, 7, 8), (qall, 8, 7), (doall, 7, 8))

    def ring_start(u, src):
        buf = rings[u][0]
        rcopy(src, buf.at[z], zsend.at[u, 0, 0], zrecv.at[u, 0, 1], dev_zr).start()
        rcopy(src, buf.at[z], zsend.at[u, 1, 0], zrecv.at[u, 1, 1], dev_zl).start()

    def serve(u, d):
        buf, reach_r, reach_l = rings[u]
        for side, reach, dev, j in (
            (0, reach_r, dev_zr, (z + NZ - d) % NZ), (1, reach_l, dev_zl, (z + d) % NZ)
        ):
            @pl.when(d <= reach)
            def _():
                rcopy(buf.at[j], buf.at[j], zsend.at[u, side, 0], zrecv.at[u, side, d], dev).wait_recv()

            @pl.when(d < reach)
            def _():
                rcopy(buf.at[j], buf.at[j], zsend.at[u, side, d], zrecv.at[u, side, d + 1], dev).start()

    def ring_end(u):
        buf, reach_r, reach_l = rings[u]

        @pl.loop(0, NZ // 2)
        def _(d):
            for side, reach, dev in ((0, reach_r, dev_zr), (1, reach_l, dev_zl)):
                @pl.when(d < reach)
                def _():
                    rcopy(buf.at[z], buf.at[z], zsend.at[u, side, d], zrecv.at[u, side, 1], dev).wait_send()

    lo, hi = pl.ds(0, HALF), pl.ds(HALF, HALF)
    for slot, dev in ((1, dev_r), (2, dev_l), (0, dev_y), (9, dev_s)):
        send(w_hbm, wall.at[f], slot, dev)
    ring_start(3, do_hbm)
    do_pair = rcopy(do_hbm, pdo, psend.at[4], precv.at[4], dev_p)
    do_pair.start()
    hid_copy = pltpu.make_async_copy(hid_hbm, hid, loc.at[0])
    own_copy = pltpu.make_async_copy(w_hbm, wall.at[f], loc.at[1])
    do_copy = pltpu.make_async_copy(do_hbm, doall.at[z], loc.at[2])
    own_copy.start()
    do_copy.start()
    hid_copy.start()

    ends = []
    total = 0
    for page in range(PAGES):
        total = total + pages[0, page]
        ends.append(total)

    def limits(pos):
        out = jnp.full(pos.shape, NYL * NZ * TOK, jnp.int32)
        for end in ends:
            out = jnp.minimum(out, jnp.where(pos < end, end, NYL * NZ * TOK))
        return out

    lane = lax.broadcasted_iota(jnp.int32, (1, TOK), 1)
    lim_q[:, :TOK] = limits(ctx * TOK + lane)
    lim_q[:, TOK:] = limits(ctx_id(1 - yl, z) * TOK + lane)

    @pl.loop(0, NZ)
    def _(j):
        lim_col[j] = limits(ctx_id(yl, j) * TOK + lane)

    mlu[0:1] = jnp.full((1, 2 * TOK), NEG, F32)
    mlu[1:8] = jnp.zeros((7, 2 * TOK), F32)

    def own(xx, yy):
        return fsdp_id(xx, yy, core)

    def sib(xx, yy):
        return fsdp_id(xx, yy, 1 - core)

    def part(shards):
        out = None
        for s in shards:
            term = nn(hid[:, pl.ds(pl.multiple_of(s * ROWS, ROWS), ROWS)], wall[s])
            out = term if out is None else out + term
        return out

    yc = 1 - yh
    serve(3, 1)
    ol, orr = wall.at[own(left, yh)], wall.at[own(right, yh)]
    arrived(ol, 1)
    on = wall.at[own(left, yh), lo]
    send(on, on, 5, dev_r)
    arrived(orr, 2)
    on = wall.at[own(right, yh), hi]
    send(on, on, 6, dev_l)
    c = wall.at[own(x, yc)]
    arrived(c, 0)
    send(c, c, 3, dev_r)
    send(c, c, 4, dev_l)
    send(ol, ol, 11, dev_s)
    send(orr, orr, 12, dev_s)
    send(c, c, 10, dev_s)
    serve(3, 2)
    hid_copy.wait()
    own_copy.wait()
    do_copy.wait()
    acc[...] = part([f, own(x, yc), own(left, yh), own(right, yh)])
    serve(3, 3)
    fa, fb = wall.at[own(far, yh), lo], wall.at[own(far, yh), hi]
    arrived(fa, 5)
    send(fa, fa, 7, dev_y)
    send(fa, fa, 15, dev_s)
    arrived(fb, 6)
    send(fb, fb, 8, dev_y)
    send(fb, fb, 16, dev_s)
    for slot, ref in (
        (9, wall.at[sib(x, yh)]), (10, wall.at[sib(x, yc)]), (11, wall.at[sib(left, yh)]),
        (12, wall.at[sib(right, yh)]),
    ):
        arrived(ref, slot)
    acc[...] += part([sib(x, yh), sib(x, yc), sib(left, yh), sib(right, yh)])
    serve(3, 4)
    cl, cr = wall.at[own(left, yc)], wall.at[own(right, yc)]
    arrived(cl, 3)
    send(cl, cl, 13, dev_s)
    arrived(cr, 4)
    send(cr, cr, 14, dev_s)
    acc[...] += part([own(left, yc), own(right, yc), own(far, yh)])
    serve(3, 5)
    ca, cb = wall.at[own(far, yc), lo], wall.at[own(far, yc), hi]
    arrived(ca, 7)
    send(ca, ca, 17, dev_s)
    arrived(cb, 8)
    send(cb, cb, 18, dev_s)
    for slot, ref in (
        (13, wall.at[sib(left, yc)]), (14, wall.at[sib(right, yc)]), (15, wall.at[sib(far, yh), lo]),
        (16, wall.at[sib(far, yh), hi]), (17, wall.at[sib(far, yc), lo]), (18, wall.at[sib(far, yc), hi]),
    ):
        arrived(ref, slot)
    acc[...] += part([own(far, yc), sib(left, yc), sib(right, yc), sib(far, yh), sib(far, yc)])
    proj[...] = acc[...].astype(BF16)
    kall[z] = proj[:, HD : 2 * HD]
    vall[z] = proj[:, 2 * HD :]
    ring_start(0, kall.at[z])
    ring_start(1, vall.at[z])
    pair = rcopy(proj, pqkv, psend.at[0], precv.at[0], dev_p)
    pair.start()
    qall[z] = proj[:, :HD]
    wall_copy = pltpu.make_async_copy(wall, wall_out, loc.at[3])
    wall_copy.start()

    q2[:TOK] = proj[:, :HD]
    do2[:TOK] = doall[z]
    do_pair.wait_recv()
    do2[TOK:] = pdo[...]
    serve(3, 6)
    pair.wait_recv()
    q2[TOK:] = pqkv[:, :HD]

    key_row = lax.broadcasted_iota(jnp.int32, (TOK, 1), 0)
    last_q = ctx_id(1, z)

    def score(j, also):
        @pl.when(also & (ctx_id(yl, j) <= last_q + REACH))
        def _():
            s = nt(kall[j], q2[...]) * SCALE
            dp = nt(vall[j], do2[...])
            s = jnp.where(ctx_id(yl, j) * TOK + key_row < lim_q[...], s, NEG)
            s_keep[j] = s
            dp_keep[j] = dp
            m = mlu[0:1]
            m_new = jnp.maximum(m, jnp.max(s, axis=0, keepdims=True))
            p = jnp.exp(s - m_new)
            a = jnp.exp(m - m_new)
            mlu[0:1] = m_new
            mlu[1:2] = mlu[1:2] * a + jnp.sum(p, axis=0, keepdims=True)
            mlu[2:3] = mlu[2:3] * a + jnp.sum(p * dp, axis=0, keepdims=True)

    @pl.loop(1, NZ // 2 + 1)
    def _(k):
        serve(0, k)
        serve(1, k)

        @pl.when(k < 3)
        def _():
            serve(3, k + 6)

        @pl.when(k == LAG)
        def _():
            ring_start(2, qall.at[z])

        @pl.when(k > LAG)
        def _():
            serve(2, k - LAG)

        @pl.loop(0, 2)
        def _(side):
            score((z + NZ - (k - 1) + 2 * (k - 1) * side) % NZ, (side == 0) | (k > 1))

    score((z + NZ // 2) % NZ, True)

    trade = rcopy(mlu, mlu_in, psend.at[1], precv.at[1], dev_p)
    trade.start()
    serve(2, NZ // 2 - LAG + 1)
    trade.wait_recv()

    def merge(mine, theirs):
        m1, m2 = mlu[0:1, mine], mlu_in[0:1, theirs]
        m = jnp.maximum(m1, m2)
        a1, a2 = jnp.exp(m1 - m), jnp.exp(m2 - m)
        l = mlu[1:2, mine] * a1 + mlu_in[1:2, theirs] * a2
        u = mlu[2:3, mine] * a1 + mlu_in[2:3, theirs] * a2
        return m + jnp.log(l), u / l

    own_q, par_q = slice(0, TOK), slice(TOK, 2 * TOK)
    lse_own, dot_own = merge(own_q, par_q)
    lse_par, dot_par = merge(par_q, own_q)
    stats[z, 0:1] = lse_own
    stats[z, 1:2] = dot_own
    stats[z, 2:8] = jnp.zeros((6, TOK), F32)

    @pl.loop(1, NZ)
    def _(i):
        rcopy(stats.at[z], stats.at[z], ssend.at[i], srecv.at[i], at_z(i)).start()

    trade.wait_send()
    mlu[0:1] = jnp.concatenate([lse_own, lse_par], axis=1)
    mlu[1:2] = jnp.concatenate([dot_own, dot_par], axis=1)
    dqt[...] = jnp.zeros((HD, 2 * TOK), F32)

    @pl.loop(0, 4)
    def _(i):
        @pl.loop(0, 4)
        def _(j4):
            j = i * 4 + j4

            @pl.when(ctx_id(yl, j) <= last_q + REACH)
            def _():
                p = jnp.exp(s_keep[j] - mlu[0:1])
                ds = (p * (dp_keep[j] - mlu[1:2]) * SCALE).astype(BF16)
                dqt[...] += tn(kall[j], ds)

        @pl.when(i < LAG - 1)
        def _():
            serve(2, NZ // 2 - LAG + 2 + i)

    out_x[...] = dqt[:, TOK:].astype(BF16)
    dq_copy = rcopy(out_x, in_x, psend.at[2], precv.at[2], dev_p)
    dq_copy.start()

    def keys(src, k_block, wait):
        dkv[...] = jnp.zeros((TOK, 2 * HD), F32)

        @pl.loop(0, NZ)
        def _(i):
            step = (i + 1) // 2
            j = (z + NZ + jnp.where(i % 2 == 1, step, -step)) % NZ
            if wait:
                @pl.when(i > 0)
                def _():
                    d = (z + NZ - j) % NZ
                    rcopy(stats.at[j], stats.at[j], ssend.at[d], srecv.at[d], dev_p).wait_recv()

            @pl.when(k_block <= ctx_id(yl, j) + REACH)
            def _():
                s = nt(src[:, HD : 2 * HD], qall[j]) * SCALE
                dp = nt(src[:, 2 * HD :], doall[j])
                s = jnp.where(k_block * TOK + key_row < lim_col[j], s, NEG)
                p = jnp.exp(s - stats[j, 0:1])
                ds = (p * (dp - stats[j, 1:2]) * SCALE).astype(BF16)
                dkv[:, :HD] += nn(ds, qall[j])
                dkv[:, HD:] += nn(p.astype(BF16), doall[j])

    keys(pqkv, ctx_id(1 - yl, z), True)
    out_kv[...] = dkv[...].astype(BF16)
    kv_copy = rcopy(out_kv, in_kv, psend.at[3], precv.at[3], dev_p)
    kv_copy.start()
    keys(proj, ctx, False)
    dq_copy.wait_recv()
    grad_qkv[:, :HD] = (dqt[:, :TOK] + in_x[...].astype(F32)).T.astype(BF16)
    kv_copy.wait_recv()
    grad_qkv[:, HD:] = (dkv[...] + in_kv[...].astype(F32)).astype(BF16)

    for copy in sent + [do_pair, pair, dq_copy, kv_copy]:
        copy.wait_send()
    for u in range(4):
        ring_end(u)

    @pl.loop(1, NZ)
    def _(d):
        rcopy(stats.at[z], stats.at[z], ssend.at[d], srecv.at[d], dev_p).wait_send()

    wall_copy.wait()


def front(pages, hidden, w, grad_out):
    n = NX * NYH * NC
    any_spec = pl.BlockSpec(memory_space=pl.ANY)
    vmem = pl.BlockSpec(memory_space=pltpu.VMEM)
    dma = pltpu.SemaphoreType.DMA
    return pl.pallas_call(
        front_kernel,
        out_shape=(
            jax.ShapeDtypeStruct((n, ROWS, QKV), BF16),
            jax.ShapeDtypeStruct((TOK, QKV), BF16),
        ),
        in_specs=[pl.BlockSpec(memory_space=pltpu.SMEM)] + [any_spec] * 3,
        out_specs=(any_spec, vmem),
        scratch_shapes=[
            pltpu.VMEM((TOK, D), BF16),
            pltpu.VMEM((n, ROWS, QKV), BF16),
            pltpu.VMEM((TOK, QKV), F32),
            pltpu.VMEM((TOK, QKV), BF16),
            pltpu.VMEM((TOK, QKV), BF16),
            pltpu.VMEM((NZ, TOK, HD), BF16),
            pltpu.VMEM((NZ, TOK, HD), BF16),
            pltpu.VMEM((NZ, TOK, HD), BF16),
            pltpu.VMEM((NZ, TOK, HD), BF16),
            pltpu.VMEM((TOK, HD), BF16),
            pltpu.VMEM((2 * TOK, HD), BF16),
            pltpu.VMEM((2 * TOK, HD), BF16),
            pltpu.VMEM((1, 2 * TOK), jnp.int32),
            pltpu.VMEM((NZ, 1, TOK), jnp.int32),
            pltpu.VMEM((NZ, TOK, 2 * TOK), F32),
            pltpu.VMEM((NZ, TOK, 2 * TOK), F32),
            pltpu.VMEM((8, 2 * TOK), F32),
            pltpu.VMEM((8, 2 * TOK), F32),
            pltpu.VMEM((NZ, 8, TOK), F32),
            pltpu.VMEM((HD, 2 * TOK), F32),
            pltpu.VMEM((TOK, 2 * HD), F32),
            pltpu.VMEM((HD, TOK), BF16),
            pltpu.VMEM((HD, TOK), BF16),
            pltpu.VMEM((TOK, 2 * HD), BF16),
            pltpu.VMEM((TOK, 2 * HD), BF16),
            dma((19,)),
            dma((19,)),
            dma((4, 2, NZ // 2)),
            dma((4, 2, NZ // 2 + 1)),
            dma((5,)),
            dma((5,)),
            dma((NZ,)),
            dma((NZ,)),
            dma((4,)),
        ],
        compiler_params=pltpu.CompilerParams(
            collective_id=0, has_side_effects=True, vmem_limit_bytes=58 << 20
        ),
        name="front",
    )(pages, hidden, w, grad_out)


PATCH = 8
SLICE = ROWS // PATCH


def reduce_kernel(
    hid_hbm, gq, gw_out,
    hid, term, sib, sib_in, got, gotb, relay, total, part, part_in, mid, mid_in, fin, loc, csend, crecv, nsend, nrecv, asend, arecv,
):
    yl, z, x, yh, core = place()
    ctx, f = ctx_id(yl, z), fsdp_id(x, yh, core)
    dev_l, dev_r, dev_y, dev_s = neighbours()
    zl, zh = z % 4, z // 4

    def patch_dev(i):
        return (ctx_id(i // 4, zh * 4 + i % 4), f)

    me = yl * 4 + zl
    peers = [(me + i) % PATCH for i in range(1, PATCH)]
    far_z = [(ctx_id(yl, (z + 4 * i) % NZ), f) for i in range(1, 4)]
    hid_copy = pltpu.make_async_copy(hid_hbm, hid, loc.at[0])
    hid_copy.start()
    greet([dev_l, dev_r, dev_y, dev_s] + [patch_dev(i) for i in peers] + far_z)
    hid_copy.wait()

    n8 = NX * NYH
    lo, hi = pl.ds(0, HALF), pl.ds(HALF, HALF)

    def block(s):
        return tn(hid[:, pl.ds(pl.multiple_of(s * ROWS, ROWS), ROWS)], gq[...])

    left, right, far = (x + NX - 1) % NX, (x + 1) % NX, (x + 2) % NX
    yc = 1 - yh

    def at(xx, yy):
        return xx * NYH + yy

    sent = []

    def send(src, dst, slot, dev):
        copy = rcopy(src, dst, nsend.at[len(sent)], nrecv.at[slot], dev)
        copy.start()
        sent.append(copy)

    def arrived(ref, slot):
        rcopy(ref, ref, nsend.at[0], nrecv.at[slot], dev_s).wait_recv()

    def up(ref):
        return ref[...].astype(F32)

    order = [
        at(far, yc), at(left, yc), at(right, yc), at(far, yh), at(x, yc), at(right, yh), at(left, yh), at(x, yh)
    ]
    for n, i in enumerate(order):
        sib[i] = block(2 * i + 1 - core).astype(BF16)
        rcopy(sib.at[i], sib_in.at[i], csend.at[n], crecv.at[n], dev_s).start()
    for n, i in enumerate(order):
        mine = block(2 * i + core)
        rcopy(sib_in.at[i], sib_in.at[i], csend.at[n], crecv.at[n], dev_s).wait_recv()
        term[i] = (mine + up(sib_in.at[i])).astype(BF16)
        if n < 3:
            to, dev = ((0, dev_y), (2, dev_l), (1, dev_r))[n]
            for h, rows in enumerate((lo, hi)):
                send(term.at[i, rows], got.at[to, rows], 2 * to + h, dev)
    t_far, t_c, t_r, t_l = at(far, yh), at(x, yc), at(right, yh), at(left, yh)
    arrived(got.at[0, lo], 0)
    relay[0, lo] = (up(term.at[t_far, lo]) + up(got.at[0, lo])).astype(BF16)
    send(relay.at[0, lo], gotb.at[0], 12, dev_r)
    arrived(got.at[0, hi], 1)
    relay[0, hi] = (up(term.at[t_far, hi]) + up(got.at[0, hi])).astype(BF16)
    send(relay.at[0, hi], gotb.at[1], 13, dev_l)
    for h, rows in enumerate((lo, hi)):
        arrived(got.at[1, rows], 2 + h)
        arrived(got.at[2, rows], 4 + h)
        relay[1, rows] = (up(term.at[t_c, rows]) + up(got.at[1, rows]) + up(got.at[2, rows])).astype(BF16)
        send(relay.at[1, rows], got.at[5, rows], 10 + h, dev_y)
        if h == 0:
            send(term.at[t_r, hi], got.at[3, hi], 7, dev_r)
            send(term.at[t_l, lo], got.at[4, lo], 8, dev_l)
    arrived(gotb.at[0], 12)
    relay[2, lo] = (up(term.at[t_r, lo]) + up(gotb.at[0])).astype(BF16)
    send(relay.at[2, lo], got.at[3, lo], 6, dev_r)
    arrived(gotb.at[1], 13)
    relay[2, hi] = (up(term.at[t_l, hi]) + up(gotb.at[1])).astype(BF16)
    send(relay.at[2, hi], got.at[4, hi], 9, dev_l)
    for h, rows in enumerate((lo, hi)):
        for slot in (3, 4, 5):
            arrived(got.at[slot, rows], 2 * slot + h)
    total[...] = up(term.at[at(x, yh)]) + up(got.at[3]) + up(got.at[4]) + up(got.at[5])
    part[...] = total[...].astype(BF16).reshape(PATCH, SLICE, QKV)

    for i in range(1, PATCH):
        to = (me + i) % PATCH
        copy = rcopy(part.at[to], part_in.at[i], asend.at[i], arecv.at[i], patch_dev(to))
        copy.start()
        sent.append(copy)
    acc = total[pl.ds(pl.multiple_of(me * SLICE, SLICE), SLICE), :]
    for i in range(1, PATCH):
        rcopy(part_in.at[i], part_in.at[i], asend.at[i], arecv.at[i], dev_s).wait_recv()
        acc += part_in[i].astype(F32)
    mid[...] = acc.astype(BF16)
    for i in range(1, 4):
        copy = rcopy(mid, mid_in.at[i], asend.at[7 + i], arecv.at[7 + i], far_z[i - 1])
        copy.start()
        sent.append(copy)
    for i in range(1, 4):
        rcopy(mid_in.at[i], mid_in.at[i], asend.at[7 + i], arecv.at[7 + i], dev_s).wait_recv()
    mid_in[0] = mid[...]
    acc = jnp.zeros((SLICE, QKV), F32)
    for h in range(4):
        acc += mid_in[(zh - h + 4) % 4].astype(F32)
    fin[me] = acc.astype(BF16)
    for i in range(1, PATCH):
        to = (me + i) % PATCH
        copy = rcopy(fin.at[me], fin.at[me], asend.at[10 + i], arecv.at[10 + i], patch_dev(to))
        copy.start()
        sent.append(copy)
    for i in range(1, PATCH):
        src = fin.at[(me + PATCH - i) % PATCH]
        rcopy(src, src, asend.at[10 + i], arecv.at[10 + i], dev_s).wait_recv()
    gw_out[...] = fin[...].reshape(ROWS, QKV).astype(F32)
    for copy in sent:
        copy.wait_send()

    @pl.loop(0, n8)
    def _(i):
        rcopy(sib.at[i], sib_in.at[i], csend.at[i], crecv.at[i], dev_s).wait_send()


def reduce_weights(hidden, gq):
    n8 = NX * NYH
    vmem = pl.BlockSpec(memory_space=pltpu.VMEM)
    dma = pltpu.SemaphoreType.DMA
    return pl.pallas_call(
        reduce_kernel,
        out_shape=jax.ShapeDtypeStruct((ROWS, QKV), F32),
        in_specs=[pl.BlockSpec(memory_space=pl.ANY), vmem],
        out_specs=vmem,
        scratch_shapes=[
            pltpu.VMEM((TOK, D), BF16),
            pltpu.VMEM((n8, ROWS, QKV), BF16),
            pltpu.VMEM((n8, ROWS, QKV), BF16),
            pltpu.VMEM((n8, ROWS, QKV), BF16),
            pltpu.VMEM((6, ROWS, QKV), BF16),
            pltpu.VMEM((2, HALF, QKV), BF16),
            pltpu.VMEM((3, ROWS, QKV), BF16),
            pltpu.VMEM((ROWS, QKV), F32),
            pltpu.VMEM((PATCH, SLICE, QKV), BF16),
            pltpu.VMEM((PATCH, SLICE, QKV), BF16),
            pltpu.VMEM((SLICE, QKV), BF16),
            pltpu.VMEM((4, SLICE, QKV), BF16),
            pltpu.VMEM((PATCH, SLICE, QKV), BF16),
            dma((1,)),
            dma((n8,)),
            dma((n8,)),
            dma((14,)),
            dma((14,)),
            dma((18,)),
            dma((18,)),
        ],
        compiler_params=pltpu.CompilerParams(
            collective_id=1, has_side_effects=True, vmem_limit_bytes=58 << 20
        ),
        name="reduce_weights",
    )(hidden, gq)


def local(hidden_in, page_tokens, grad_attn, w_qkv):
    hidden = hidden_in[0]
    wall, gq = front(page_tokens, hidden, w_qkv, grad_attn[0])
    grad_w = reduce_weights(hidden, gq)
    grad_hidden = nt(gq, wall.reshape(D, QKV)).astype(BF16)[None]
    return grad_hidden, grad_w


def solution(mesh):
    in_specs = (P("fsdp", "ctx", None), P("fsdp", None), P("fsdp", "ctx", None), P("fsdp", None))
    out_specs = (P("fsdp", "ctx", None), P("fsdp", None))
    return jax.shard_map(local, mesh=mesh, in_specs=in_specs, out_specs=out_specs, check_vma=False)
```

time: 179 us -> 150 us (0.84)
  Pallas kernels: 171 us -> 143 us
  local copies, waits for them, and re-layouts: 4.75 us -> 1.77 us
  matrix products: 2.61 us -> 4.61 us
    pallas_call x2 -> x1, Pallas kernels: 122 us -> 95.6 us  [front(): pl.pallas_call(front_kernel, out_shape=(jax.ShapeDtypeStruct((n, ROWS, QK...]
    unnamed x11 -> x1, local copies, waits for them, and re-layouts: 4.75 us -> 1.77 us
    dot_general x1, matrix products: 2.61 us -> 4.61 us  [nt(): lax.dot_general(a, b, (((1,), (1,)), ((), ())), preferred_element_type=F32)]
where the time goes in v2:
time: 150 us
  Pallas kernels  143 us (95%)
  matrix products  4.61 us (3%)
  local copies, waits for them, and re-layouts  1.77 us (1%)
    pallas_call x1, Pallas kernels, front(): pl.pallas_call(front_kernel, out_shape=(jax.ShapeDtypeStruct((n, ROWS, QK...  95.6 us
    pallas_call x1, Pallas kernels, reduce_weights(): pl.pallas_call(reduce_kernel, out_shape=jax.ShapeDtypeStruct((ROWS, QKV),...  46.9 us
    dot_general x1, matrix products, nt(): lax.dot_general(a, b, (((1,), (1,)), ((), ())), preferred_element_type=F32)  4.61 us

profile of v2, /device:TPU:6, one launch (start us, length us, event | category | flops | bytes accessed | tf_op | source)
XLA Modules:
  0.0 149.6 jit_solution(2006935487049115731)
XLA Ops:
  0.6 95.6 %front.1 = (bf16[16,256,384]{2,1,0:T(8,128)(2,1)}, bf16[256,384]{1,0:T(8,128)(2,1)}) custom-call(s32[1,16]{1,0:T(1,128)} %pages.1, bf16[256,4096]{1,0:T(8,128)(2,1)} %bitcast.7, bf16[256,384]{1,0:T(8,128)(2,1)} %w_hbm.1, bf16[256,128]{1,0:T(8,128)(2,1)} %bitcast.10), custom_call_target="tpu_custom_call" | custom-call | tf_op jit(solution)/shard_map/front/pallas_call | solution.py:392
  96.3 4.6 %fusion = bf16[1,256,4096]{2,1,0:T(8,128)(2,1)} fusion(bf16[256,384]{1,0:T(8,128)(2,1)} %get-tuple-element.4.gq, bf16[4096,384]{1,0:T(8,128)(2,1)} %bitcast.9), kind=kOutput, calls=%fused_computation.1 | convolution fusion | flops 806354944 | bytes 5439488 | tf_op jit(solution)/shard_map/dot_general | solution.py:51
  100.9 46.9 %reduce_weights.1 = f32[256,384]{1,0:T(8,128)} custom-call(bf16[256,4096]{1,0:T(8,128)(2,1)} %bitcast.8, bf16[256,384]{1,0:T(8,128)(2,1)} %get-tuple-element.4.gq), custom_call_target="tpu_custom_call" | custom-call | tf_op jit(solution)/shard_map/reduce_weights/pallas_call | solution.py:575
  147.8 1.8 %copy.7 = f32[256,384]{1,0:T(8,128)} copy(f32[256,384]{1,0:T(8,128)} %reduce_weights.1) | data formatting | bytes 786432

commit v3 on v2

v3 whole, which is shorter than its diff:
```python
import functools

import jax
import jax.numpy as jnp
from jax import lax
from jax.experimental import pallas as pl
from jax.experimental.pallas import tpu as pltpu
from jax.sharding import PartitionSpec as P

MESH = pl.DeviceIdType.MESH
F32, BF16 = jnp.float32, jnp.bfloat16
NX, NYH, NC, NYL, NZ = 4, 2, 2, 2, 16
TOK, HD, D = 256, 128, 4096
QKV = 3 * HD
ROWS = D // (NX * NYH * NC)
NEG = -1e30
SCALE = HD ** -0.5
LOG2E = 1.4426950408889634
SCALE2 = SCALE * LOG2E
REACH = 5
HALF = TOK // 2
PAGES = 16
LAG = 2
PATCH = 8
SLICE = ROWS // PATCH


def fsdp_id(x, yh, core):
    return (x * NYH + yh) * NC + core


def ctx_id(yl, z):
    return yl * NZ + z


def place():
    ctx, f = lax.axis_index("ctx"), lax.axis_index("fsdp")
    return ctx // NZ, ctx % NZ, f // (NYH * NC), (f // NC) % NYH, f % NC


def rcopy(src, dst, send, recv, dev):
    return pltpu.make_async_remote_copy(
        src_ref=src, dst_ref=dst, send_sem=send, recv_sem=recv, device_id=dev, device_id_type=MESH
    )


def greet(peers):
    barrier = pltpu.get_barrier_semaphore()
    for dev in peers:
        pl.semaphore_signal(barrier, inc=1, device_id=dev, device_id_type=MESH)
    pl.semaphore_wait(barrier, len(peers))


def nt(a, b):
    return lax.dot_general(a, b, (((1,), (1,)), ((), ())), preferred_element_type=F32)


def tn(a, b):
    return lax.dot_general(a, b, (((0,), (0,)), ((), ())), preferred_element_type=F32)


def nn(a, b):
    return jnp.dot(a, b, preferred_element_type=F32)


def neighbours():
    yl, z, x, yh, core = place()
    ctx, f = ctx_id(yl, z), fsdp_id(x, yh, core)
    left, right = (x + NX - 1) % NX, (x + 1) % NX
    dev_l, dev_r = (ctx, fsdp_id(left, yh, core)), (ctx, fsdp_id(right, yh, core))
    dev_y = (ctx_id(1 - yl, z), fsdp_id(x, 1 - yh, core))
    dev_s = (ctx, fsdp_id(x, yh, 1 - core))
    return dev_l, dev_r, dev_y, dev_s


def step_kernel(
    pages, hid_hbm, w_hbm, do_hbm, ghid_out, gw_out,
    hid, wall, acc, proj, pk, pv, kall, vall, qall, doall, pdo, q2, do2, lim_q, lim_col, s_keep, dp_keep, mlu, mlu_in,
    stats, dqt, dkv, out_x, in_x, out_kv, in_kv, wsend, wrecv, zsend, zrecv, psend, precv, ssend, srecv, loc,
    gq, hid_t, ghid, term, sbuf, sbuf_in, got, gotb, relay, total, prt, prt_in, mid, mid_in, fin, csend, crecv, nsend, nrecv, asend, arecv,
):
    yl, z, x, yh, core = place()
    ctx, f = ctx_id(yl, z), fsdp_id(x, yh, core)
    left, right, far = (x + NX - 1) % NX, (x + 1) % NX, (x + 2) % NX
    dev_l, dev_r, dev_y, dev_s = neighbours()
    dev_p = (ctx_id(1 - yl, z), f)

    def at_z(d):
        return (ctx_id(yl, (z + d) % NZ), f)

    dev_zl, dev_zr = at_z(NZ - 1), at_z(1)
    greet([dev_l, dev_r, dev_y, dev_s, dev_p, dev_zl, dev_zr])

    sent = []

    def send(src, dst, slot, dev):
        copy = rcopy(src, dst, wsend.at[len(sent)], wrecv.at[slot], dev)
        copy.start()
        sent.append(copy)

    def arrived(ref, slot):
        rcopy(ref, ref, wsend.at[0], wrecv.at[slot], dev_s).wait_recv()

    rings = ((kall, 8, 7), (vall, 7, 8), (qall, 8, 7), (doall, 7, 8))

    def ring_start(u, src):
        buf = rings[u][0]
        rcopy(src, buf.at[z], zsend.at[u, 0, 0], zrecv.at[u, 0, 1], dev_zr).start()
        rcopy(src, buf.at[z], zsend.at[u, 1, 0], zrecv.at[u, 1, 1], dev_zl).start()

    def serve(u, d):
        buf, reach_r, reach_l = rings[u]
        for side, reach, dev, j in (
            (0, reach_r, dev_zr, (z + NZ - d) % NZ), (1, reach_l, dev_zl, (z + d) % NZ)
        ):
            @pl.when(d <= reach)
            def _():
                rcopy(buf.at[j], buf.at[j], zsend.at[u, side, 0], zrecv.at[u, side, d], dev).wait_recv()

            @pl.when(d < reach)
            def _():
                rcopy(buf.at[j], buf.at[j], zsend.at[u, side, d], zrecv.at[u, side, d + 1], dev).start()

    def ring_end(u):
        buf, reach_r, reach_l = rings[u]

        @pl.loop(0, NZ // 2)
        def _(d):
            for side, reach, dev in ((0, reach_r, dev_zr), (1, reach_l, dev_zl)):
                @pl.when(d < reach)
                def _():
                    rcopy(buf.at[z], buf.at[z], zsend.at[u, side, d], zrecv.at[u, side, 1], dev).wait_send()

    lo, hi = pl.ds(0, HALF), pl.ds(HALF, HALF)
    for slot, rows, dev in ((1, lo, dev_r), (2, hi, dev_l), (19, hi, dev_r), (20, lo, dev_l)):
        send(w_hbm.at[rows], wall.at[f, rows], slot, dev)
    send(w_hbm, wall.at[f], 0, dev_y)
    send(w_hbm, wall.at[f], 9, dev_s)
    ring_start(3, do_hbm)
    do_pair = rcopy(do_hbm, pdo, psend.at[4], precv.at[4], dev_p)
    do_pair.start()
    hid_copy = pltpu.make_async_copy(hid_hbm, hid, loc.at[0])
    own_copy = pltpu.make_async_copy(w_hbm, wall.at[f], loc.at[1])
    do_copy = pltpu.make_async_copy(do_hbm, doall.at[z], loc.at[2])
    own_copy.start()
    do_copy.start()
    hid_copy.start()

    ends = []
    end = 0
    for page in range(PAGES):
        end = end + pages[0, page]
        ends.append(end)

    def limits(pos):
        out = jnp.full(pos.shape, NYL * NZ * TOK, jnp.int32)
        for stop in ends:
            out = jnp.minimum(out, jnp.where(pos < stop, stop, NYL * NZ * TOK))
        return out

    lane = lax.broadcasted_iota(jnp.int32, (1, TOK), 1)
    lim_q[:, :TOK] = limits(ctx * TOK + lane)
    lim_q[:, TOK:] = limits(ctx_id(1 - yl, z) * TOK + lane)

    @pl.loop(0, NZ)
    def _(j):
        lim_col[j] = limits(ctx_id(yl, j) * TOK + lane)

    mlu[0:1] = jnp.full((1, 2 * TOK), NEG, F32)
    mlu[1:8] = jnp.zeros((7, 2 * TOK), F32)

    def own(xx, yy):
        return fsdp_id(xx, yy, core)

    def sib(xx, yy):
        return fsdp_id(xx, yy, 1 - core)

    def project(shards):
        out = None
        for s in shards:
            term = nn(hid[:, pl.ds(pl.multiple_of(s * ROWS, ROWS), ROWS)], wall[s])
            out = term if out is None else out + term
        return out

    yc = 1 - yh
    serve(3, 1)
    ol, orr = wall.at[own(left, yh)], wall.at[own(right, yh)]
    on = wall.at[own(left, yh), lo]
    arrived(on, 1)
    send(on, on, 5, dev_r)
    on = wall.at[own(right, yh), hi]
    arrived(on, 2)
    send(on, on, 6, dev_l)
    c = wall.at[own(x, yc)]
    arrived(c, 0)
    send(c, c, 3, dev_r)
    send(c, c, 4, dev_l)
    arrived(wall.at[own(left, yh), hi], 19)
    send(ol, ol, 11, dev_s)
    arrived(wall.at[own(right, yh), lo], 20)
    send(orr, orr, 12, dev_s)
    send(c, c, 10, dev_s)
    serve(3, 2)
    hid_copy.wait()
    own_copy.wait()
    do_copy.wait()
    acc[...] = project([f, own(x, yc), own(left, yh), own(right, yh)])
    fa, fb = wall.at[own(far, yh), lo], wall.at[own(far, yh), hi]
    arrived(fa, 5)
    send(fa, fa, 7, dev_y)
    send(fa, fa, 15, dev_s)
    arrived(fb, 6)
    send(fb, fb, 8, dev_y)
    send(fb, fb, 16, dev_s)
    serve(3, 3)
    for slot, ref in (
        (9, wall.at[sib(x, yh)]), (10, wall.at[sib(x, yc)]), (11, wall.at[sib(left, yh)]),
        (12, wall.at[sib(right, yh)]),
    ):
        arrived(ref, slot)
    acc[...] += project([sib(x, yh), sib(x, yc), sib(left, yh), sib(right, yh)])
    serve(3, 4)
    cl, cr = wall.at[own(left, yc)], wall.at[own(right, yc)]
    arrived(cl, 3)
    send(cl, cl, 13, dev_s)
    arrived(cr, 4)
    send(cr, cr, 14, dev_s)
    acc[...] += project([own(left, yc), own(right, yc), own(far, yh)])
    ca, cb = wall.at[own(far, yc), lo], wall.at[own(far, yc), hi]
    arrived(ca, 7)
    send(ca, ca, 17, dev_s)
    arrived(cb, 8)
    send(cb, cb, 18, dev_s)
    for slot, ref in (
        (13, wall.at[sib(left, yc)]), (14, wall.at[sib(right, yc)]), (15, wall.at[sib(far, yh), lo]),
        (16, wall.at[sib(far, yh), hi]), (17, wall.at[sib(far, yc), lo]), (18, wall.at[sib(far, yc), hi]),
    ):
        arrived(ref, slot)
    acc[...] += project([own(far, yc), sib(left, yc), sib(right, yc), sib(far, yh), sib(far, yc)])
    proj[...] = acc[...].astype(BF16)
    kall[z] = proj[:, HD : 2 * HD]
    vall[z] = proj[:, 2 * HD :]
    ring_start(0, kall.at[z])
    ring_start(1, vall.at[z])
    qall[z] = proj[:, :HD]
    pair_q = rcopy(qall.at[z], q2.at[pl.ds(TOK, TOK)], psend.at[0], precv.at[0], dev_p)
    pair_q.start()
    pair_k = rcopy(kall.at[z], pk, psend.at[5], precv.at[5], dev_p)
    pair_k.start()
    pair_v = rcopy(vall.at[z], pv, psend.at[6], precv.at[6], dev_p)
    pair_v.start()
    q2[:TOK] = proj[:, :HD]
    do2[:TOK] = doall[z]
    serve(3, 5)

    key_row = lax.broadcasted_iota(jnp.int32, (TOK, 1), 0)
    last_q = ctx_id(1, z)

    def score(j, also):
        @pl.when(also & (ctx_id(yl, j) <= last_q + REACH))
        def _():
            s = nt(kall[j], q2[...]) * SCALE2
            dp = nt(vall[j], do2[...])
            s = jnp.where(ctx_id(yl, j) * TOK + key_row < lim_q[...], s, NEG)
            s_keep[j] = s
            dp_keep[j] = dp
            m = mlu[0:1]
            m_new = jnp.maximum(m, jnp.max(s, axis=0, keepdims=True))
            p = jnp.exp2(s - m_new)
            a = jnp.exp2(m - m_new)
            mlu[0:1] = m_new
            mlu[1:2] = mlu[1:2] * a + jnp.sum(p, axis=0, keepdims=True)
            mlu[2:3] = mlu[2:3] * a + jnp.sum(p * dp, axis=0, keepdims=True)

    @pl.loop(1, NZ // 2 + 1)
    def _(k):
        serve(0, k)
        serve(1, k)

        @pl.when(k < 4)
        def _():
            serve(3, k + 5)

        @pl.when(k == 1)
        def _():
            do_pair.wait_recv()
            do2[TOK:] = pdo[...]
            pair_q.wait_recv()

        @pl.when(k == LAG)
        def _():
            ring_start(2, qall.at[z])

        @pl.when(k > LAG)
        def _():
            serve(2, k - LAG)

        @pl.loop(0, 2)
        def _(side):
            score((z + NZ - (k - 1) + 2 * (k - 1) * side) % NZ, (side == 0) | (k > 1))
            n = 2 * (k - 1) + side
            hid_t[n] = hid[:, pl.ds(pl.multiple_of(n * ROWS, ROWS), ROWS)].T

    score((z + NZ // 2) % NZ, True)

    trade = rcopy(mlu, mlu_in, psend.at[1], precv.at[1], dev_p)
    trade.start()
    serve(2, NZ // 2 - LAG + 1)
    trade.wait_recv()

    def merge(mine, theirs):
        m1, m2 = mlu[0:1, mine], mlu_in[0:1, theirs]
        m = jnp.maximum(m1, m2)
        a1, a2 = jnp.exp2(m1 - m), jnp.exp2(m2 - m)
        l = mlu[1:2, mine] * a1 + mlu_in[1:2, theirs] * a2
        u = mlu[2:3, mine] * a1 + mlu_in[2:3, theirs] * a2
        return m + jnp.log(l) * LOG2E, u / l

    own_q, par_q = slice(0, TOK), slice(TOK, 2 * TOK)
    lse_own, dot_own = merge(own_q, par_q)
    lse_par, dot_par = merge(par_q, own_q)
    stats[z, :, :TOK] = lse_own
    stats[z, :, TOK:] = dot_own

    @pl.loop(1, NZ)
    def _(i):
        rcopy(stats.at[z], stats.at[z], ssend.at[i], srecv.at[i], at_z(i)).start()

    trade.wait_send()
    mlu[0:1] = jnp.concatenate([lse_own, lse_par], axis=1)
    mlu[1:2] = jnp.concatenate([dot_own, dot_par], axis=1)
    dqt[...] = jnp.zeros((HD, 2 * TOK), F32)

    @pl.loop(0, NZ // 4)
    def _(i):
        @pl.when(ctx_id(yl, 4 * i) <= last_q + REACH)
        def _():
            for n in range(1, 4):
                @pl.when(ctx_id(yl, 4 * i + n) > last_q + REACH)
                def _():
                    s_keep[4 * i + n] = jnp.full((TOK, 2 * TOK), NEG, F32)
                    dp_keep[4 * i + n] = jnp.zeros((TOK, 2 * TOK), F32)

            out = []
            for n in range(4):
                j = 4 * i + n
                p = jnp.exp2(s_keep[j] - mlu[0:1])
                ds = (p * (dp_keep[j] - mlu[1:2])).astype(BF16)
                out.append(tn(kall[j], ds))
            dqt[...] += (out[0] + out[1]) + (out[2] + out[3])

        @pl.when((i == 1) & (LAG > 1))
        def _():
            serve(2, NZ // 2)

    dqt[...] = dqt[...] * SCALE
    out_x[...] = dqt[:, TOK:].astype(BF16)
    dq_copy = rcopy(out_x, in_x, psend.at[2], precv.at[2], dev_p)
    dq_copy.start()

    def keys(k_src, v_src, k_block, wait):
        dkv[...] = jnp.zeros((TOK, 2 * HD), F32)

        def arrive(j):
            n = (z + NZ - j) % NZ
            rcopy(stats.at[j], stats.at[j], ssend.at[n], srecv.at[n], dev_p).wait_recv()

        def work(blocks):
            seen = k_block <= ctx_id(yl, blocks[0]) + REACH
            for j in blocks[1:]:
                seen = seen | (k_block <= ctx_id(yl, j) + REACH)

            @pl.when(seen)
            def _():
                dk, dv = [], []
                for j in blocks:
                    s = nt(k_src[...], qall[j]) * SCALE2
                    dp = nt(v_src[...], doall[j])
                    s = jnp.where(k_block * TOK + key_row < lim_col[j], s, NEG)
                    p = jnp.exp2(s - stats[j, :, :TOK])
                    ds = (p * (dp - stats[j, :, TOK:])).astype(BF16)
                    dk.append(nn(ds, qall[j]))
                    dv.append(nn(p.astype(BF16), doall[j]))
                dkv[:, :HD] += sum(dk[1:], dk[0])
                dkv[:, HD:] += sum(dv[1:], dv[0])

        work([z])

        @pl.loop(0, NZ // 4 - 1)
        def _(i):
            near = [(z + NZ - 2 * i - 1) % NZ, (z + 2 * i + 1) % NZ, (z + NZ - 2 * i - 2) % NZ, (z + 2 * i + 2) % NZ]
            if wait:
                for j in near:
                    arrive(j)
            work(near)

        last = [(z + NZ // 2 + 1) % NZ, (z + NZ // 2 - 1) % NZ, (z + NZ // 2) % NZ]
        if wait:
            for j in last:
                arrive(j)
        work(last)
        dkv[:, :HD] = dkv[:, :HD] * SCALE

    pair_k.wait_recv()
    pair_v.wait_recv()
    keys(pk, pv, ctx_id(1 - yl, z), True)
    out_kv[...] = dkv[...].astype(BF16)
    kv_copy = rcopy(out_kv, in_kv, psend.at[3], precv.at[3], dev_p)
    kv_copy.start()
    dq_copy.wait_recv()
    gq[:, :HD] = (dqt[:, :TOK] + in_x[...].astype(F32)).T.astype(BF16)
    keys(kall.at[z], vall.at[z], ctx, False)
    kv_copy.wait_recv()
    gq[:, HD:] = (dkv[...] + in_kv[...].astype(F32)).astype(BF16)

    zl, zh = z % 4, z // 4

    def patch_dev(i):
        return (ctx_id(i // 4, zh * 4 + i % 4), f)

    me = yl * 4 + zl
    far_z = [(ctx_id(yl, (z + 4 * i) % NZ), f) for i in range(1, 4)]

    n8 = NX * NYH

    def grad_in(first):
        for s in range(first, first + 4):
            ghid[:, s * ROWS : (s + 1) * ROWS] = nt(gq[...], wall[s]).astype(BF16)
        cols = pl.ds(first * ROWS, 4 * ROWS)
        pltpu.make_async_copy(ghid.at[:, cols], ghid_out.at[:, cols], loc.at[3 + first // 4]).start()

    def block(s):
        return nn(hid_t[s], gq[...])

    def at(xx, yy):
        return xx * NYH + yy

    rsent = []

    def rsend(src, dst, slot, dev):
        copy = rcopy(src, dst, nsend.at[len(rsent)], nrecv.at[slot], dev)
        copy.start()
        rsent.append(copy)

    def rarrived(ref, slot):
        rcopy(ref, ref, nsend.at[0], nrecv.at[slot], dev_s).wait_recv()

    def up(ref):
        return ref[...].astype(F32)

    order = [
        at(far, yc), at(left, yc), at(right, yc), at(far, yh), at(x, yc), at(right, yh), at(left, yh), at(x, yh)
    ]
    for n, i in enumerate(order):
        sbuf[i] = block(2 * i + 1 - core).astype(BF16)
        rcopy(sbuf.at[i], sbuf_in.at[i], csend.at[n], crecv.at[n], dev_s).start()
    for n, i in enumerate(order):
        mine = block(2 * i + core)
        rcopy(sbuf_in.at[i], sbuf_in.at[i], csend.at[n], crecv.at[n], dev_s).wait_recv()
        term[i] = (mine + up(sbuf_in.at[i])).astype(BF16)
        if n < 3:
            to, dev = ((0, dev_y), (2, dev_l), (1, dev_r))[n]
            for h, rows in enumerate((lo, hi)):
                rsend(term.at[i, rows], got.at[to, rows], 2 * to + h, dev)
    grad_in(0)
    t_far, t_c, t_r, t_l = at(far, yh), at(x, yc), at(right, yh), at(left, yh)
    rarrived(got.at[0, lo], 0)
    relay[0, lo] = (up(term.at[t_far, lo]) + up(got.at[0, lo])).astype(BF16)
    rsend(relay.at[0, lo], gotb.at[0], 12, dev_r)
    rarrived(got.at[0, hi], 1)
    relay[0, hi] = (up(term.at[t_far, hi]) + up(got.at[0, hi])).astype(BF16)
    rsend(relay.at[0, hi], gotb.at[1], 13, dev_l)
    for h, rows in enumerate((lo, hi)):
        rarrived(got.at[1, rows], 2 + h)
        rarrived(got.at[2, rows], 4 + h)
        relay[1, rows] = (up(term.at[t_c, rows]) + up(got.at[1, rows]) + up(got.at[2, rows])).astype(BF16)
        rsend(relay.at[1, rows], got.at[5, rows], 10 + h, dev_y)
        if h == 0:
            rsend(term.at[t_r, hi], got.at[3, hi], 7, dev_r)
            rsend(term.at[t_l, lo], got.at[4, lo], 8, dev_l)
    rarrived(gotb.at[0], 12)
    relay[2, lo] = (up(term.at[t_r, lo]) + up(gotb.at[0])).astype(BF16)
    rsend(relay.at[2, lo], got.at[3, lo], 6, dev_r)
    rarrived(gotb.at[1], 13)
    relay[2, hi] = (up(term.at[t_l, hi]) + up(gotb.at[1])).astype(BF16)
    rsend(relay.at[2, hi], got.at[4, hi], 9, dev_l)
    for h, rows in enumerate((lo, hi)):
        for slot in (3, 4, 5):
            rarrived(got.at[slot, rows], 2 * slot + h)
    total[...] = up(term.at[at(x, yh)]) + up(got.at[3]) + up(got.at[4]) + up(got.at[5])
    prt[...] = total[...].astype(BF16).reshape(PATCH, SLICE, QKV)

    for i in range(1, PATCH):
        to = (me + i) % PATCH
        copy = rcopy(prt.at[to], prt_in.at[i], asend.at[i], arecv.at[i], patch_dev(to))
        copy.start()
        rsent.append(copy)
    grad_in(4)
    run = total[pl.ds(pl.multiple_of(me * SLICE, SLICE), SLICE), :]
    for i in range(1, PATCH):
        rcopy(prt_in.at[i], prt_in.at[i], asend.at[i], arecv.at[i], dev_s).wait_recv()
        run += prt_in[i].astype(F32)
    mid[...] = run.astype(BF16)
    for i in range(1, 4):
        copy = rcopy(mid, mid_in.at[i], asend.at[7 + i], arecv.at[7 + i], far_z[i - 1])
        copy.start()
        rsent.append(copy)
    grad_in(8)
    for i in range(1, 4):
        rcopy(mid_in.at[i], mid_in.at[i], asend.at[7 + i], arecv.at[7 + i], dev_s).wait_recv()
    mid_in[0] = mid[...]
    run = jnp.zeros((SLICE, QKV), F32)
    for h in range(4):
        run += mid_in[(zh - h + 4) % 4].astype(F32)
    fin[me] = run.astype(BF16)
    for i in range(1, PATCH):
        to = (me + i) % PATCH
        copy = rcopy(fin.at[me], fin.at[me], asend.at[10 + i], arecv.at[10 + i], patch_dev(to))
        copy.start()
        rsent.append(copy)
    grad_in(12)
    for i in range(1, PATCH):
        src = fin.at[(me + PATCH - i) % PATCH]
        rcopy(src, src, asend.at[10 + i], arecv.at[10 + i], dev_s).wait_recv()
    gw_out[...] = fin[...].reshape(ROWS, QKV).astype(F32)
    for copy in sent + rsent + [do_pair, pair_q, pair_k, pair_v, dq_copy, kv_copy]:
        copy.wait_send()
    for u in range(4):
        ring_end(u)

    @pl.loop(1, NZ)
    def _(d):
        rcopy(stats.at[z], stats.at[z], ssend.at[d], srecv.at[d], dev_p).wait_send()

    @pl.loop(0, n8)
    def _(i):
        rcopy(sbuf.at[i], sbuf_in.at[i], csend.at[i], crecv.at[i], dev_s).wait_send()

    for first in range(0, NX * NYH * NC, 4):
        cols = pl.ds(first * ROWS, 4 * ROWS)
        pltpu.make_async_copy(ghid.at[:, cols], ghid_out.at[:, cols], loc.at[3 + first // 4]).wait()


def step(pages, hidden, w, grad_out):
    n, n8 = NX * NYH * NC, NX * NYH
    hbm = pl.BlockSpec(memory_space=pltpu.HBM)
    vmem = pl.BlockSpec(memory_space=pltpu.VMEM)
    dma = pltpu.SemaphoreType.DMA
    return pl.pallas_call(
        step_kernel,
        out_shape=(
            jax.ShapeDtypeStruct((TOK, D), BF16),
            jax.ShapeDtypeStruct((ROWS, QKV), F32),
        ),
        in_specs=[pl.BlockSpec(memory_space=pltpu.SMEM)] + [hbm] * 3,
        out_specs=(hbm, vmem),
        scratch_shapes=[
            pltpu.VMEM((TOK, D), BF16),
            pltpu.VMEM((n, ROWS, QKV), BF16),
            pltpu.VMEM((TOK, QKV), F32),
            pltpu.VMEM((TOK, QKV), BF16),
            pltpu.VMEM((TOK, HD), BF16),
            pltpu.VMEM((TOK, HD), BF16),
            pltpu.VMEM((NZ, TOK, HD), BF16),
            pltpu.VMEM((NZ, TOK, HD), BF16),
            pltpu.VMEM((NZ, TOK, HD), BF16),
            pltpu.VMEM((NZ, TOK, HD), BF16),
            pltpu.VMEM((TOK, HD), BF16),
            pltpu.VMEM((2 * TOK, HD), BF16),
            pltpu.VMEM((2 * TOK, HD), BF16),
            pltpu.VMEM((1, 2 * TOK), jnp.int32),
            pltpu.VMEM((NZ, 1, TOK), jnp.int32),
            pltpu.VMEM((NZ, TOK, 2 * TOK), F32),
            pltpu.VMEM((NZ, TOK, 2 * TOK), F32),
            pltpu.VMEM((8, 2 * TOK), F32),
            pltpu.VMEM((8, 2 * TOK), F32),
            pltpu.VMEM((NZ, 1, 2 * TOK), F32),
            pltpu.VMEM((HD, 2 * TOK), F32),
            pltpu.VMEM((TOK, 2 * HD), F32),
            pltpu.VMEM((HD, TOK), BF16),
            pltpu.VMEM((HD, TOK), BF16),
            pltpu.VMEM((TOK, 2 * HD), BF16),
            pltpu.VMEM((TOK, 2 * HD), BF16),
            dma((21,)),
            dma((21,)),
            dma((4, 2, NZ // 2)),
            dma((4, 2, NZ // 2 + 1)),
            dma((7,)),
            dma((7,)),
            dma((NZ,)),
            dma((NZ,)),
            dma((7,)),
            pltpu.VMEM((TOK, QKV), BF16),
            pltpu.VMEM((n, ROWS, TOK), BF16),
            pltpu.VMEM((TOK, D), BF16),
            pltpu.VMEM((n8, ROWS, QKV), BF16),
            pltpu.VMEM((n8, ROWS, QKV), BF16),
            pltpu.VMEM((n8, ROWS, QKV), BF16),
            pltpu.VMEM((6, ROWS, QKV), BF16),
            pltpu.VMEM((2, HALF, QKV), BF16),
            pltpu.VMEM((3, ROWS, QKV), BF16),
            pltpu.VMEM((ROWS, QKV), F32),
            pltpu.VMEM((PATCH, SLICE, QKV), BF16),
            pltpu.VMEM((PATCH, SLICE, QKV), BF16),
            pltpu.VMEM((SLICE, QKV), BF16),
            pltpu.VMEM((4, SLICE, QKV), BF16),
            pltpu.VMEM((PATCH, SLICE, QKV), BF16),
            dma((n8,)),
            dma((n8,)),
            dma((14,)),
            dma((14,)),
            dma((18,)),
            dma((18,)),
        ],
        compiler_params=pltpu.CompilerParams(
            collective_id=0, has_side_effects=True, vmem_limit_bytes=60 << 20
        ),
        name="step",
    )(pages, hidden, w, grad_out)


def local(hidden_in, page_tokens, grad_attn, w_qkv):
    grad_hidden, grad_w = step(page_tokens, hidden_in[0], w_qkv, grad_attn[0])
    return grad_hidden[None], grad_w


def solution(mesh):
    in_specs = (P("fsdp", "ctx", None), P("fsdp", None), P("fsdp", "ctx", None), P("fsdp", None))
    out_specs = (P("fsdp", "ctx", None), P("fsdp", None))
    return jax.shard_map(local, mesh=mesh, in_specs=in_specs, out_specs=out_specs, check_vma=False)
```

time: 150 us -> 128 us (0.85)
  Pallas kernels: 143 us -> 122 us
  matrix products: 4.61 us -> 0 us
  local copies, waits for them, and re-layouts: 1.77 us -> 3.93 us
    pallas_call x2 -> x1, Pallas kernels: 143 us -> 122 us  [step(): pl.pallas_call(step_kernel, out_shape=(jax.ShapeDtypeStruct((TOK, D), BF1...]
    dot_general x1 -> x0, matrix products: 4.61 us -> none  [nt(): lax.dot_general(a, b, (((1,), (1,)), ((), ())), preferred_element_type=F32)]
    unnamed x1 -> x4, local copies, waits for them, and re-layouts: 1.77 us -> 3.93 us
where the time goes in v3:
time: 128 us; the launch traced here: 126 us
  Pallas kernels  122 us (95%)
  local copies, waits for them, and re-layouts  3.93 us (3%)
    pallas_call x1, Pallas kernels, step(): pl.pallas_call(step_kernel, out_shape=(jax.ShapeDtypeStruct((TOK, D), BF1...  122 us
    unnamed x4, local copies, waits for them, and re-layouts  3.93 us

profile of v3, /device:TPU:6, one launch (start us, length us, event | category | flops | bytes accessed | tf_op | source)
XLA Modules:
  0.0 126.3 jit_solution(14342381549480010157)
XLA Ops:
  0.6 121.7 %step.1 = (bf16[256,4096]{1,0:T(8,128)(2,1)}, f32[256,384]{1,0:T(8,128)}) custom-call(s32[1,16]{1,0:T(1,128)} %pages.1, bf16[256,4096]{1,0:T(8,128)(2,1)} %bitcast.3, bf16[256,384]{1,0:T(8,128)(2,1)} %w_hbm.1, bf16[256,128]{1,0:T(8,128)(2,1)} %bitcast.5), custom_call_target="tpu_custom_call" | custom-call | tf_op jit(solution)/shard_map/step/pallas_call | solution.py:549
  122.3 0.0 copy-start
  122.3 3.2 %copy.8 = bf16[1,256,4096]{2,1,0:T(8,128)(2,1)} copy(bf16[1,256,4096]{2,1,0:T(8,128)(2,1)} %bitcast.4) | data formatting | bytes 4194304
  125.5 0.0 copy-done
  125.5 0.7 copy.9
Async XLA Ops:
  122.3 3.2 %copy-start = (f32[256,384]{1,0:T(8,128)S(1)}, f32[256,384]{1,0:T(8,128)}, u32[]{:S(2)}) copy-start(f32[256,384]{1,0:T(8,128)} %get-tuple-element.9) | copy-start | bytes 1179652

commit v4 on v3

--- a/solution.py
+++ b/solution.py
@@ -18,6 +18,7 @@
 LOG2E = 1.4426950408889634
 SCALE2 = SCALE * LOG2E
 REACH = 5
+WRITES = 8
 HALF = TOK // 2
 PAGES = 16
 LAG = 2
@@ -448,6 +449,11 @@
     def up(ref):
         return ref[...].astype(F32)
 
+    turns = (0, 2, 1, 3)
+
+    def quarter(q):
+        return pl.ds(q * (HALF // 2), HALF // 2)
+
     order = [
         at(far, yc), at(left, yc), at(right, yc), at(far, yh), at(x, yc), at(right, yh), at(left, yh), at(x, yh)
     ]
@@ -458,35 +464,37 @@
         mine = block(2 * i + core)
         rcopy(sbuf_in.at[i], sbuf_in.at[i], csend.at[n], crecv.at[n], dev_s).wait_recv()
         term[i] = (mine + up(sbuf_in.at[i])).astype(BF16)
-        if n < 3:
-            to, dev = ((0, dev_y), (2, dev_l), (1, dev_r))[n]
+        if n == 0:
+            for q in turns:
+                rsend(term.at[i, quarter(q)], got.at[0, quarter(q)], q, dev_y)
+        elif n < 3:
+            to, dev = ((2, dev_l), (1, dev_r))[n - 1]
             for h, rows in enumerate((lo, hi)):
-                rsend(term.at[i, rows], got.at[to, rows], 2 * to + h, dev)
+                rsend(term.at[i, rows], got.at[to, rows], 2 + 2 * to + h, dev)
     grad_in(0)
     t_far, t_c, t_r, t_l = at(far, yh), at(x, yc), at(right, yh), at(left, yh)
-    rarrived(got.at[0, lo], 0)
-    relay[0, lo] = (up(term.at[t_far, lo]) + up(got.at[0, lo])).astype(BF16)
-    rsend(relay.at[0, lo], gotb.at[0], 12, dev_r)
-    rarrived(got.at[0, hi], 1)
-    relay[0, hi] = (up(term.at[t_far, hi]) + up(got.at[0, hi])).astype(BF16)
-    rsend(relay.at[0, hi], gotb.at[1], 13, dev_l)
+    for q in turns:
+        rows, dev = quarter(q), (dev_r, dev_l)[q // 2]
+        rarrived(got.at[0, rows], q)
+        relay[0, rows] = (up(term.at[t_far, rows]) + up(got.at[0, rows])).astype(BF16)
+        rsend(relay.at[0, rows], gotb.at[rows], 12 + q, dev)
     for h, rows in enumerate((lo, hi)):
-        rarrived(got.at[1, rows], 2 + h)
-        rarrived(got.at[2, rows], 4 + h)
+        rarrived(got.at[1, rows], 4 + h)
+        rarrived(got.at[2, rows], 6 + h)
         relay[1, rows] = (up(term.at[t_c, rows]) + up(got.at[1, rows]) + up(got.at[2, rows])).astype(BF16)
-        rsend(relay.at[1, rows], got.at[5, rows], 10 + h, dev_y)
+        rsend(relay.at[1, rows], got.at[5, rows], 8 + h, dev_y)
         if h == 0:
-            rsend(term.at[t_r, hi], got.at[3, hi], 7, dev_r)
-            rsend(term.at[t_l, lo], got.at[4, lo], 8, dev_l)
-    rarrived(gotb.at[0], 12)
-    relay[2, lo] = (up(term.at[t_r, lo]) + up(gotb.at[0])).astype(BF16)
-    rsend(relay.at[2, lo], got.at[3, lo], 6, dev_r)
-    rarrived(gotb.at[1], 13)
-    relay[2, hi] = (up(term.at[t_l, hi]) + up(gotb.at[1])).astype(BF16)
-    rsend(relay.at[2, hi], got.at[4, hi], 9, dev_l)
-    for h, rows in enumerate((lo, hi)):
-        for slot in (3, 4, 5):
-            rarrived(got.at[slot, rows], 2 * slot + h)
+            rsend(term.at[t_r, hi], got.at[3, hi], 10, dev_r)
+            rsend(term.at[t_l, lo], got.at[4, lo], 11, dev_l)
+    for q in turns:
+        rows, dev, mine, to = quarter(q), (dev_r, dev_l)[q // 2], (t_r, t_l)[q // 2], 3 + q // 2
+        rarrived(gotb.at[rows], 12 + q)
+        relay[2, rows] = (up(term.at[mine, rows]) + up(gotb.at[rows])).astype(BF16)
+        rsend(relay.at[2, rows], got.at[to, rows], 16 + q, dev)
+    for ref, slot in ((got.at[5, lo], 8), (got.at[5, hi], 9), (got.at[3, hi], 10), (got.at[4, lo], 11)):
+        rarrived(ref, slot)
+    for q in turns:
+        rarrived(got.at[3 + q // 2, quarter(q)], 16 + q)
     total[...] = up(term.at[at(x, yh)]) + up(got.at[3]) + up(got.at[4]) + up(got.at[5])
     prt[...] = total[...].astype(BF16).reshape(PATCH, SLICE, QKV)
 
@@ -597,7 +605,7 @@
             pltpu.VMEM((n8, ROWS, QKV), BF16),
             pltpu.VMEM((n8, ROWS, QKV), BF16),
             pltpu.VMEM((6, ROWS, QKV), BF16),
-            pltpu.VMEM((2, HALF, QKV), BF16),
+            pltpu.VMEM((ROWS, QKV), BF16),
             pltpu.VMEM((3, ROWS, QKV), BF16),
             pltpu.VMEM((ROWS, QKV), F32),
             pltpu.VMEM((PATCH, SLICE, QKV), BF16),
@@ -607,8 +615,8 @@
             pltpu.VMEM((PATCH, SLICE, QKV), BF16),
             dma((n8,)),
             dma((n8,)),
-            dma((14,)),
-            dma((14,)),
+            dma((20,)),
+            dma((20,)),
             dma((18,)),
             dma((18,)),
         ],
@@ -619,8 +627,47 @@
     )(pages, hidden, w, grad_out)
 
 
+def write_kernel(ghid, gw, ghid_out, gw_out, buf, buf_w, sem_in, sem_out):
+    rows = TOK // WRITES
+    legs = [
+        (
+            pltpu.make_async_copy(src, via, sem_in.at[i]),
+            pltpu.make_async_copy(via, dst, sem_out.at[i]),
+        )
+        for i, (src, via, dst) in enumerate(
+            [(gw, buf_w, gw_out)]
+            + [tuple(ref.at[pl.ds(i * rows, rows)] for ref in (ghid, buf, ghid_out)) for i in range(WRITES)]
+        )
+    ]
+    for fetch, _ in legs:
+        fetch.start()
+    for fetch, store in legs:
+        fetch.wait()
+        store.start()
+    for _, store in legs:
+        store.wait()
+
+
+def write(ghid, gw):
+    any_spec = pl.BlockSpec(memory_space=pl.ANY)
+    return pl.pallas_call(
+        write_kernel,
+        out_shape=(jax.ShapeDtypeStruct(ghid.shape, BF16), jax.ShapeDtypeStruct(gw.shape, F32)),
+        in_specs=[any_spec] * 2,
+        out_specs=(any_spec, any_spec),
+        scratch_shapes=[
+            pltpu.VMEM(ghid.shape, BF16),
+            pltpu.VMEM(gw.shape, F32),
+            pltpu.SemaphoreType.DMA((WRITES + 1,)),
+            pltpu.SemaphoreType.DMA((WRITES + 1,)),
+        ],
+        compiler_params=pltpu.CompilerParams(vmem_limit_bytes=60 << 20),
+        name="write",
+    )(ghid, gw)
+
+
 def local(hidden_in, page_tokens, grad_attn, w_qkv):
-    grad_hidden, grad_w = step(page_tokens, hidden_in[0], w_qkv, grad_attn[0])
+    grad_hidden, grad_w = write(*step(page_tokens, hidden_in[0], w_qkv, grad_attn[0]))
     return grad_hidden[None], grad_w
 
 

time: 128 us -> 125 us (0.977); the launches traced: 126 us -> 125 us
  local copies, waits for them, and re-layouts: 3.93 us -> 0 us
  Pallas kernels: 122 us -> 124 us
    unnamed x4 -> x0, local copies, waits for them, and re-layouts: 3.93 us -> none
    pallas_call x0 -> x1, Pallas kernels: none -> 2.59 us  [write(): pl.pallas_call(write_kernel, out_shape=(jax.ShapeDtypeStruct(ghid.shape,...]
where the time goes in v4:
time: 125 us
  Pallas kernels  124 us (99%)
    pallas_call x1, Pallas kernels, step(): pl.pallas_call(step_kernel, out_shape=(jax.ShapeDtypeStruct((TOK, D), BF1...  122 us
    pallas_call x1, Pallas kernels, write(): pl.pallas_call(write_kernel, out_shape=(jax.ShapeDtypeStruct(ghid.shape,...  2.59 us

profile of v4, /device:TPU:6, one launch (start us, length us, event | category | flops | bytes accessed | tf_op | source)
XLA Modules:
  0.0 124.8 jit_solution(922282170196981578)
XLA Ops:
  0.6 121.6 %step.1 = (bf16[256,4096]{1,0:T(8,128)(2,1)}, f32[256,384]{1,0:T(8,128)}) custom-call(s32[1,16]{1,0:T(1,128)} %pages.1, bf16[256,4096]{1,0:T(8,128)(2,1)} %bitcast.3, bf16[256,384]{1,0:T(8,128)(2,1)} %w_hbm.1, bf16[256,128]{1,0:T(8,128)(2,1)} %bitcast.4), custom_call_target="tpu_custom_call" | custom-call | tf_op jit(solution)/shard_map/step/pallas_call | solution.py:557
  122.2 2.6 %write.1 = (bf16[256,4096]{1,0:T(8,128)(2,1)}, f32[256,384]{1,0:T(8,128)}) custom-call(bf16[256,4096]{1,0:T(8,128)(2,1)} %get-tuple-element.6.ghid, f32[256,384]{1,0:T(8,128)} %get-tuple-element.7.gw), custom_call_target="tpu_custom_call" | custom-call | tf_op jit(solution)/shard_map/write/pallas_call | solution.py:653

commit v5 on v4

--- a/solution.py
+++ b/solution.py
@@ -371,19 +371,26 @@
             for j in blocks[1:]:
                 seen = seen | (k_block <= ctx_id(yl, j) + REACH)
 
-            @pl.when(seen)
-            def _():
+            edge = k_block >= ctx_id(yl, blocks[0])
+            for j in blocks[1:]:
+                edge = edge | (k_block >= ctx_id(yl, j))
+
+            def tiles(masked):
                 dk, dv = [], []
                 for j in blocks:
                     s = nt(k_src[...], qall[j]) * SCALE2
                     dp = nt(v_src[...], doall[j])
-                    s = jnp.where(k_block * TOK + key_row < lim_col[j], s, NEG)
+                    if masked:
+                        s = jnp.where(k_block * TOK + key_row < lim_col[j], s, NEG)
                     p = jnp.exp2(s - stats[j, :, :TOK])
                     ds = (p * (dp - stats[j, :, TOK:])).astype(BF16)
                     dk.append(nn(ds, qall[j]))
                     dv.append(nn(p.astype(BF16), doall[j]))
                 dkv[:, :HD] += sum(dk[1:], dk[0])
                 dkv[:, HD:] += sum(dv[1:], dv[0])
+
+            pl.when(seen & edge)(lambda: tiles(True))
+            pl.when(seen & jnp.logical_not(edge))(lambda: tiles(False))
 
         work([z])
 

time: 125 us -> 126 us (level); the launches traced: 125 us -> 124 us
  no operation moved by 1% of the time
where the time goes in v5:
time: 126 us; the launch traced here: 124 us
  Pallas kernels  124 us (98%)
    pallas_call x1, Pallas kernels, step(): pl.pallas_call(step_kernel, out_shape=(jax.ShapeDtypeStruct((TOK, D), BF1...  121 us
    pallas_call x1, Pallas kernels, write(): pl.pallas_call(write_kernel, out_shape=(jax.ShapeDtypeStruct(ghid.shape,...  2.59 us

profile of v5, /device:TPU:6, one launch (start us, length us, event | category | flops | bytes accessed | tf_op | source)
XLA Modules:
  0.0 124.4 jit_solution(5077035641641891509)
XLA Ops:
  0.6 121.0 %step.1 = (bf16[256,4096]{1,0:T(8,128)(2,1)}, f32[256,384]{1,0:T(8,128)}) custom-call(s32[1,16]{1,0:T(1,128)} %pages.1, bf16[256,4096]{1,0:T(8,128)(2,1)} %bitcast.3, bf16[256,384]{1,0:T(8,128)(2,1)} %w_hbm.1, bf16[256,128]{1,0:T(8,128)(2,1)} %bitcast.4), custom_call_target="tpu_custom_call" | custom-call | tf_op jit(solution)/shard_map/step/pallas_call | solution.py:564
  121.7 2.6 %write.1 = (bf16[256,4096]{1,0:T(8,128)(2,1)}, f32[256,384]{1,0:T(8,128)}) custom-call(bf16[256,4096]{1,0:T(8,128)(2,1)} %get-tuple-element.6.ghid, f32[256,384]{1,0:T(8,128)} %get-tuple-element.7.gw), custom_call_target="tpu_custom_call" | custom-call | tf_op jit(solution)/shard_map/write/pallas_call | solution.py:660
